TPU v7x, 32 devices: a whole 2x2x4 slice. The times are simulated.
32 devices in a mesh: vocab: 4 (over z), rows: 8 (over y, x, core).
Axes of the slice: x: 2, y: 2, z: 4, core: 2. Of those that a mesh axis runs over, the one named last changes fastest.
Arguments:
- trunk_hidden: bfloat16 [32, 7168], P('rows'), may hold values from -8 to 8
- mtp_state: bfloat16 [32, 7168], P('rows'), may hold values from -24 to 24, as said below
- mtp_gain: bfloat16 [7168], replicated, may hold values from 0.099609375 to 1.8984375
- head_weight: bfloat16 [4608, 7168], P(('vocab', 'rows')), may hold values from -0.28347335 to 0.28347335, as said below
- target_ids: int32 [32], replicated, may hold values from 0 to 4607
- mtp_target_ids: int32 [32], replicated, may hold values from 0 to 4607
- attn_values: bfloat16 [32, 16, 128], P('rows'), may hold values from -6 to 6
- out_proj: bfloat16 [2048, 7168], P('rows', 'vocab'), may hold values from -0.125 to 0.125
Outputs:
- grad_trunk: bfloat16 [32, 7168], P('rows')
- grad_residual: bfloat16 [32, 7168], P('rows')
- grad_gain: float32 [7168], replicated
- grad_head: bfloat16 [4608, 7168], P(('vocab', 'rows'))
- grad_attn: bfloat16 [32, 16, 128], P('vocab', 'rows')
- grad_out_proj: bfloat16 [2048, 7168], P('rows', 'vocab')
Inputs may be any that keep to these rules, and one draw needn't show every extreme that they name: `mtp_state`: block outputs; rows differ in scale. `head_weight`: head rows.
All inputs are finite; a program needn't handle non-finite values.
Results may differ from a plain program's by a relative error of at most 0.025.
Values may be sent and summed in bfloat16 or wider, within the bound.
No kernel may reach another device: no remote copies, remote signals or barrier semaphores. Data moves between devices by JAX's collectives and lax.ppermute only.
A program may use at most 64 MiB of HBM per device.

v0:
```python
import functools

import jax
import jax.numpy as jnp
from jax import lax
from jax.experimental import pallas as pl
from jax.experimental.pallas import tpu as pltpu
from jax.sharding import PartitionSpec as P

loss_scale = 8.0
mtp_share = 0.3
norm_eps = 1e-06


def swap(x, axis, k):
    n = lax.axis_size(axis)
    return lax.ppermute(x, axis, [(i, i ^ k) for i in range(n)])


def tree_sum(parts):
    while len(parts) > 1:
        parts = [a + b for a, b in zip(parts[::2], parts[1::2])]
    return parts[0]


def plain(
    trunk_hidden,
    mtp_state,
    mtp_gain,
    head_weight,
    target_ids,
    mtp_target_ids,
    attn_values,
    out_proj,
):
    f32, bf16 = jnp.float32, jnp.bfloat16
    tok, width = trunk_hidden.shape
    nrow = lax.axis_size("rows")
    nvoc = lax.axis_size("vocab")
    ndev = nrow * nvoc
    nchip = nrow // 2
    row = lax.axis_index("rows")
    voc = lax.axis_index("vocab")
    core = row & 1
    chip = row >> 1
    vrows = head_weight.shape[0]
    cols = out_proj.shape[1]
    hdim = out_proj.shape[0]
    ntok = nrow * tok
    gain = mtp_gain.astype(f32)

    stacked = jnp.concatenate([trunk_hidden, mtp_state], axis=0)
    gathered = lax.all_gather(stacked, "rows", axis=0, tiled=True).reshape(nrow, 2, tok, width)
    state = gathered[:, 1].astype(f32)
    inverse = lax.rsqrt(jnp.mean(state * state, axis=-1, keepdims=True) + norm_eps)
    mtp_hidden = (state * inverse * gain).astype(bf16)
    hidden = jnp.stack([gathered[:, 0], mtp_hidden], axis=1).reshape(2 * ntok, width)

    targets = jnp.stack(
        [target_ids.reshape(nrow, tok), mtp_target_ids.reshape(nrow, tok)], axis=1
    ).reshape(-1)
    shares = jnp.broadcast_to(
        jnp.array([loss_scale, loss_scale * mtp_share], f32)[None, :, None], (nrow, 2, tok)
    ).reshape(-1)
    vocab_ids = (voc * nrow + row) * vrows + jnp.arange(vrows, dtype=jnp.int32)
    onehot = targets[:, None] == vocab_ids[None, :]

    logits = lax.dot_general(
        hidden, head_weight, (((1,), (1,)), ((), ())), preferred_element_type=f32
    )
    peak = jnp.max(logits, axis=1)
    below = logits - peak[:, None]
    weight = jnp.exp(below)
    mass = jnp.sum(weight, axis=1)
    moment = jnp.sum(weight * below, axis=1)
    picked = jnp.sum(jnp.where(onehot, logits, 0.0), axis=1)
    stats = jnp.stack([peak, mass, moment, picked])
    everyone = lax.all_to_all(
        jnp.broadcast_to(stats[None], (ndev,) + stats.shape),
        ("vocab", "rows"),
        split_axis=0,
        concat_axis=0,
        tiled=True,
    )
    peaks, masses, moments, picks = (everyone[:, k] for k in range(4))
    top = jnp.max(peaks, axis=0)
    drop = peaks - top
    factor = jnp.exp(drop)
    total = jnp.sum(factor * masses, axis=0)
    spread = jnp.sum(factor * (moments + drop * masses), axis=0) / total
    dot_mean = shares * (spread - (jnp.sum(picks, axis=0) - top)) / width
    dot_mean = dot_mean.reshape(nrow, 2, tok)[:, 1].reshape(ntok, 1)

    logit_grads = (
        shares[:, None] * (jnp.exp(logits - top[:, None]) / total[:, None] - onehot.astype(f32))
    ).astype(bf16)

    by_core = logit_grads.reshape(nchip, 2, 2, tok, vrows)

    def rows_for(which):
        part = lax.dynamic_index_in_dim(by_core, which, 1, keepdims=False)
        own = [lax.dynamic_index_in_dim(part, chip ^ j, 0, keepdims=False)[0] for j in range(nchip)]
        return jnp.concatenate([part[:, 1].reshape(nchip * tok, vrows)] + own, axis=0)

    def grads_of(rows):
        return jnp.dot(rows, head_weight, preferred_element_type=f32).astype(bf16)

    away = grads_of(rows_for(1 - core))
    kept = grads_of(rows_for(core))
    pair = (kept.astype(f32) + swap(away, "rows", 1).astype(f32)).astype(bf16)

    def columns_for(k):
        return lax.dynamic_slice_in_dim(pair, (voc ^ k) * cols, cols, 1)

    column_sum = tree_sum(
        [columns_for(0).astype(f32)]
        + [swap(columns_for(k), "vocab", k).astype(f32) for k in range(1, nvoc)]
    ).astype(bf16)
    nmod = nchip * tok
    module, main = column_sum[:nmod], column_sum[nmod:].reshape(nchip, tok, cols)
    plane = [jnp.concatenate([module, main[0]], axis=0)] + [
        swap(jnp.concatenate([module, main[j]], axis=0), "rows", 2 * j) for j in range(1, nchip)
    ]
    plane_sum = tree_sum([part.astype(f32) for part in plane]).astype(bf16)
    module, trunk_piece = plane_sum[:nmod], plane_sum[nmod:]
    other = swap(module, "rows", 1)

    grad_head = lax.dot_general(
        logit_grads, hidden, (((0,), (0,)), ((), ())), preferred_element_type=f32
    ).astype(bf16)
    values = lax.all_to_all(attn_values, "rows", split_axis=1, concat_axis=0, tiled=True)
    values = values.reshape(ntok, hdim)

    first = jnp.where(core == 0, module, other).reshape(nchip, 1, tok, cols)
    second = jnp.where(core == 0, other, module).reshape(nchip, 1, tok, cols)
    mtp_grad = jnp.concatenate([first, second], axis=1).reshape(ntok, cols).astype(f32)
    inv = inverse.reshape(ntok, 1)
    normed = lax.dynamic_slice_in_dim(
        gathered[:, 1].reshape(ntok, width), voc * cols, cols, 1
    ).astype(f32) * inv
    gain_piece = jnp.sum(mtp_grad * normed, axis=0, keepdims=True)
    scaled = mtp_grad * lax.dynamic_slice_in_dim(gain, voc * cols, cols, 0)
    residual = (inv * (scaled - normed * dot_mean)).astype(bf16)
    attn_terms = lax.dot_general(
        residual, out_proj, (((1,), (1,)), ((), ())), preferred_element_type=f32
    ).astype(bf16)
    grad_out_proj = lax.dot_general(
        values, residual, (((0,), (0,)), ((), ())), preferred_element_type=f32
    ).astype(bf16)

    residual_piece = lax.dynamic_slice_in_dim(residual, row * tok, tok, 0)
    gain_high = gain_piece.astype(bf16)
    gain_low = (gain_piece - gain_high.astype(f32)).astype(bf16)
    tok_voc = ntok // nvoc
    lines = -(-tok_voc * hdim // cols)
    terms = attn_terms.reshape(nvoc, tok_voc * hdim)
    terms = jnp.pad(terms, ((0, 0), (0, lines * cols - tok_voc * hdim))).reshape(nvoc, lines, cols)
    shared = jnp.concatenate([trunk_piece, residual_piece, gain_high, gain_low], axis=0)

    def parcel(k):
        mine = lax.dynamic_index_in_dim(terms, voc ^ k, 0, keepdims=False)
        return jnp.concatenate([shared, mine], axis=0)

    parcels = [parcel(0)] + [swap(parcel(k), "vocab", k) for k in range(1, nvoc)]
    ordered = jnp.stack(parcels)
    grad_attn = jnp.sum(ordered[:, 2 * tok + 2 :].astype(f32), axis=0).astype(bf16)
    grad_attn = grad_attn.reshape(-1)[: tok_voc * hdim].reshape(
        tok_voc, hdim // attn_values.shape[2], attn_values.shape[2]
    )
    pieces = [
        lax.dynamic_index_in_dim(ordered, voc ^ k, 0, keepdims=False)[: 2 * tok + 2]
        for k in range(nvoc)
    ]
    whole = jnp.concatenate(pieces, axis=1)
    grad_trunk = whole[:tok]
    grad_residual = whole[tok : 2 * tok]
    grad_gain = whole[2 * tok].astype(f32) + whole[2 * tok + 1].astype(f32)
    return (grad_trunk, grad_residual, grad_gain, grad_head, grad_attn, grad_out_proj)


NT = (((1,), (1,)), ((), ()))
NN = (((1,), (0,)), ((), ()))


def iota(shape, dim):
    return lax.broadcasted_iota(jnp.int32, shape, dim)


def matmul(a, b, dims=NN):
    return lax.dot_general(a, b, dims, preferred_element_type=jnp.float32)


def onehot(mask):
    return jnp.where(mask, 1.0, 0.0).astype(jnp.bfloat16)


def chunks(width):
    step = next(s for s in (1024, 512, 256, 128) if width % s == 0)
    return [slice(c, c + step) for c in range(0, width, step)]


def kernel_call(body, outs, *args, side=None, away=()):
    vmem, hbm = pl.BlockSpec(memory_space=pltpu.VMEM), pl.BlockSpec(memory_space=pltpu.HBM)
    return pl.pallas_call(
        body,
        in_specs=[hbm if k in away else vmem for k in range(len(args))],
        out_specs=[vmem] * len(outs),
        out_shape=[jax.ShapeDtypeStruct(s, d) for s, d in outs],
        scratch_shapes=side or [],
        compiler_params=pltpu.CompilerParams(vmem_limit_bytes=16 << 20),
    )(*args)


def module_lines(half, rows, tok):
    line, spot = iota((half, rows), 0), iota((half, rows), 1)
    owner = line // tok
    block = (owner % 2 ^ lax.axis_index("rows") % 2) * (half // tok // 2) + owner // 2
    return spot == block * 2 * tok + tok + line % tok


def in_order(near, tok, half):
    pick = module_lines(half, near.shape[1], tok)
    return jnp.sum(jnp.where(pick, near, 0.0), axis=1, keepdims=True)


def across(column):
    eye = iota((column.shape[0],) * 2, 0) == iota((column.shape[0],) * 2, 1)
    return jnp.sum(jnp.where(eye, column, 0.0), axis=0, keepdims=True)


def vocab_rows(vrows):
    row = lax.axis_index("rows")
    base = lax.axis_index("vocab") * lax.axis_size("rows")
    line = iota((2 * vrows, 1), 0)
    own = line < vrows
    return jnp.where(own, (base + row) * vrows + line, (base + (row ^ 1)) * vrows + line - vrows)


def prepare_kernel(tok, w_src, gain_src, ids_ref, mids_ref, w_ref, gain_ref, tgt_ref):
    f32 = jnp.float32
    w_ref[...] = w_src[...]
    gains = gain_src[...].astype(f32)
    for k in range(gains.shape[0]):
        gain_ref[:, k * 128 : (k + 1) * 128] = gains[k : k + 1]
    half, rows = ids_ref.shape[1], tgt_ref.shape[1]
    eye = iota((half, half), 0) == iota((half, half), 1)
    main = jnp.sum(jnp.where(eye, ids_ref[...], 0), axis=1, keepdims=True)
    other = jnp.sum(jnp.where(eye, mids_ref[...], 0), axis=1, keepdims=True)
    src, dst = iota((half, rows), 0), iota((half, rows), 1)
    own = src // tok % 2 == lax.axis_index("rows") % 2
    place = src // tok // 2 * 2 * tok + src % tok
    tgt = jnp.where(own & (dst == place), main, 0) + jnp.where(own & (dst == place + tok), other, 0)
    tgt_ref[...] = jnp.sum(tgt, axis=0, keepdims=True)


def inverse_of(x_ref, at):
    width = x_ref.shape[1]
    square = sum(jnp.square(x_ref[at, c].astype(jnp.float32)) for c in chunks(width))
    return lax.rsqrt(jnp.sum(square, axis=1, keepdims=True) / width + norm_eps)


def head_kernel(tok, count, *refs):
    f32, bf16 = jnp.float32, jnp.bfloat16
    blocks, (w_ref, part_ref, gain_ref, tgt_ref) = refs[:count], refs[count : count + 4]
    raw_ref, hid_ref, lt_ref, inv_ref, msg_ref = refs[count + 4 :]
    size, width = blocks[0].shape
    rows, vrows = count * size, w_ref.shape[0]
    chip = lax.axis_index("rows") // 2
    module = iota((size, 1), 0) // tok % 2 == 1
    inverses = [inverse_of(block, slice(None)) for block in blocks]
    places = [pl.ds(pl.multiple_of((chip ^ k) * size, size), size) for k in range(count)]
    for k in range(count):
        inv_ref[places[k]] = inverses[k]
    own = jnp.zeros((vrows, rows), f32)
    other = jnp.zeros((vrows, rows), f32)
    for c in chunks(width):
        gain = gain_ref[:, c]
        for k, block in enumerate(blocks):
            raw = block[:, c]
            x = raw.astype(f32)
            raw_ref[places[k], c] = raw
            hid_ref[places[k], c] = jnp.where(module, x * inverses[k] * gain, x).astype(bf16)
        h = hid_ref[:, c]
        own += matmul(w_ref[:, c], h, NT)
        other += matmul(part_ref[:, c], h, NT)
    lt = jnp.concatenate([own, other], axis=0)
    lt_ref[...] = lt
    peak = jnp.max(lt, axis=0, keepdims=True)
    below = lt - peak
    weight = jnp.exp(below)
    picked = jnp.where(vocab_rows(vrows) == tgt_ref[...], lt, 0.0)
    for k, stat in enumerate(
        (
            peak,
            jnp.sum(weight, axis=0, keepdims=True),
            jnp.sum(weight * below, axis=0, keepdims=True),
            jnp.sum(picked, axis=0, keepdims=True),
        )
    ):
        msg_ref[:, k * rows : (k + 1) * rows] = jnp.broadcast_to(stat, (msg_ref.shape[0], rows))


def loss_kernel(tok, nvoc, ev_ref, lt_ref, tgt_ref, w_ref, part_ref, own_ref, away_ref, dot_ref, *outs):
    f32, bf16 = jnp.float32, jnp.bfloat16
    vrows, width = w_ref.shape
    rows = lt_ref.shape[1]
    row, voc = lax.axis_index("rows"), lax.axis_index("vocab")
    core, chip = row % 2, row // 2
    module = (iota((1, rows), 1) // tok) % 2 == 1
    share = jnp.where(module, loss_scale * mtp_share, loss_scale).astype(f32)
    peaks, masses, moments, picks = (ev_ref[:, k * rows : (k + 1) * rows] for k in range(4))
    sender = iota((ev_ref.shape[0], 1), 0) % 2

    def combine(which):
        mine = sender == which
        top = jnp.max(jnp.where(mine, peaks, -jnp.inf), axis=0, keepdims=True)
        drop = jnp.where(mine, peaks - top, 0.0)
        factor = jnp.where(mine, jnp.exp(drop), 0.0)
        total = jnp.sum(factor * masses, axis=0, keepdims=True)
        spread = jnp.sum(factor * (moments + drop * masses), axis=0, keepdims=True) / total
        picked = jnp.sum(jnp.where(mine, picks, 0.0), axis=0, keepdims=True)
        return top, total, share * (spread - (picked - top)) / width

    top, total, dot_own = combine(core)
    dot_other = combine(1 - core)[2]
    dot_ref[...] = in_order(jnp.concatenate([dot_own, dot_other], axis=1), tok, dot_ref.shape[0])
    hit = jnp.where(vocab_rows(vrows) == tgt_ref[...], 1.0, 0.0)
    gt = (share * (jnp.exp(lt_ref[...] - top) / total - hit)).astype(bf16)
    own_ref[...] = gt[:vrows]
    away_ref[...] = gt[vrows:]
    column, main = outs[:nvoc], outs[nvoc:]
    half = rows // 2
    line, col = iota((rows, rows), 0), iota((rows, rows), 1)
    spot = line % half
    want = jnp.where(
        line < half, spot // tok * 2 * tok + tok, (spot // tok ^ chip) * 2 * tok
    )
    pick = onehot(col == want + spot % tok)
    grads = matmul(pick, gt[:vrows], NT).astype(bf16)
    others = matmul(pick, gt[vrows:], NT).astype(bf16)
    cols = width // nvoc
    for k in range(nvoc):
        at = pl.ds(pl.multiple_of((voc ^ k) * cols, 128), cols)
        total = matmul(grads, w_ref[:, at]) + matmul(others, part_ref[:, at])
        column[k][...] = total[:half].astype(bf16)
        for j, out in enumerate(main):
            out[:, at] = total[half + j * tok : half + (j + 1) * tok].astype(bf16)


def rest_kernel(tok, raw_ref, gain_ref, hid_ref, own_ref, got_ref, hid_out, gt_out, inv_out):
    f32, bf16 = jnp.float32, jnp.bfloat16
    rows, width = raw_ref.shape
    module = (iota((rows, 1), 0) // tok) % 2 == 1
    inverse = inverse_of(raw_ref, slice(None))
    inv_out[...] = inverse
    for c in chunks(width):
        x = raw_ref[:, c].astype(f32)
        hid_out[:rows, c] = hid_ref[:, c]
        hid_out[rows:, c] = jnp.where(module, x * inverse * gain_ref[:, c], x).astype(bf16)
    gt_out[:, :rows] = own_ref[...]
    gt_out[:, rows:] = got_ref[...]


def column_kernel(nvoc, attn_ref, *refs):
    f32, bf16 = jnp.float32, jnp.bfloat16
    parts, outs = refs[:nvoc], refs[nvoc:]
    _, cols = parts[0].shape
    chip = lax.axis_index("rows") // 2
    total = tree_sum([p[...].astype(f32) for p in parts]).astype(bf16)
    tok, heads, _ = attn_ref.shape
    each = heads // len(outs)
    line, spot = iota((each, heads), 0), iota((each, heads), 1)
    for j, out in enumerate(outs):
        out[:, :cols] = total
        pick = onehot(spot == (chip ^ j) * each + line)
        tail = jnp.concatenate([matmul(pick, attn_ref[i]) for i in range(tok)], axis=0)
        out[:, cols:] = tail.astype(bf16)


def main_kernel(*refs):
    for c in chunks(refs[-1].shape[1]):
        refs[-1][:, c] = tree_sum([m[:, c].astype(jnp.float32) for m in refs[:-1]]).astype(
            jnp.bfloat16
        )


def plane_kernel(tok, nchip, hold_ref, *refs):
    f32, bf16 = jnp.float32, jnp.bfloat16
    parts, (swap_ref, val_ref) = refs[:nchip], refs[nchip:]
    nmod, hdim = val_ref.shape
    size = parts[0].shape[1] - swap_ref.shape[1] + hdim
    cols = swap_ref.shape[1] - hdim
    each, heads = parts[0].shape[0] // tok, hdim // size
    swap_ref[:, :cols] = tree_sum([p[:, :cols].astype(f32) for p in parts]).astype(bf16)
    held = jnp.concatenate([p[:, cols:].astype(f32) for p in parts], axis=0).astype(bf16)
    core = lax.axis_index("rows") % 2
    line, spot = iota((nmod, held.shape[0]), 0), iota((nmod, held.shape[0]), 1)
    for h in range(heads):
        at = line * each + h
        lanes = slice(h * size, (h + 1) * size)
        val_ref[:, lanes] = matmul(onehot(spot == at + core * heads), held).astype(bf16)
        away = matmul(onehot(spot == at + (1 - core) * heads), held)
        swap_ref[:, cols + h * size : cols + (h + 1) * size] = away.astype(bf16)


def last_kernel(
    tok, raw_ref, part_ref, inv_ref, far_ref, dot_ref, gain_ref, proj_ref, own_ref, other_ref, val_ref, res_ref, val_out, *outs
):
    f32, bf16 = jnp.float32, jnp.bfloat16
    parcels, (scratch,) = outs[:-1], outs[-1:]
    half = raw_ref.shape[0]
    rows = 2 * half
    hdim, cols = proj_ref.shape
    nmod = own_ref.shape[0]
    nvoc = len(parcels)
    row, voc = lax.axis_index("rows"), lax.axis_index("vocab")
    core, chip = row % 2, row // 2
    line, spot = iota((half, nmod), 0), iota((half, nmod), 1)
    owner = line // tok
    same = spot == (owner // 2) * tok + line % tok
    grad = matmul(onehot(same & (owner % 2 == core)), own_ref[:, :cols])
    grad += matmul(onehot(same & (owner % 2 != core)), other_ref[:, :cols])
    start = pl.multiple_of(voc * cols, 128)
    near = jnp.concatenate([across(inv_ref[...]), across(far_ref[...])], axis=1)
    inverse = in_order(near, tok, half)
    at = pl.ds(start, cols)
    state = jnp.concatenate([raw_ref[:, at], part_ref[:, at]], axis=0)
    normed = matmul(onehot(module_lines(half, rows, tok)), state) * inverse
    gain_piece = jnp.sum(grad * normed, axis=0, keepdims=True)
    gain = gain_ref[:, pl.ds(start, cols)]
    scaled = grad * gain
    residual = (inverse * (scaled - normed * dot_ref[...])).astype(bf16)
    res_ref[...] = residual
    scratch[...] = matmul(residual, proj_ref[...], NT)
    tok_voc = half // nvoc
    fold = tok_voc // tok
    strip = cols // fold
    line, spot = iota((tok_voc, half), 0), iota((tok_voc, half), 1)
    mine = sum(
        matmul(
            onehot((line // tok == f) & (spot == row * tok + line % tok)),
            residual[:, f * strip : (f + 1) * strip],
        )
        for f in range(fold)
    ).astype(bf16)
    pieces = [gain_piece[:, c : c + hdim] for c in range(0, cols, hdim)]
    pieces += [jnp.zeros((1, hdim), f32)] * (tok_voc - len(pieces))
    gains = jnp.concatenate(pieces, axis=0)
    high = gains.astype(bf16)
    low = (gains - high.astype(f32)).astype(bf16)
    for k, out in enumerate(parcels):
        block = scratch[pl.ds(pl.multiple_of((voc ^ k) * tok_voc, tok_voc), tok_voc), :]
        out[:, :strip] = mine
        out[:, strip : strip + hdim] = block.astype(bf16)
        out[:, strip + hdim : strip + 2 * hdim] = high
        out[:, strip + 2 * hdim :] = low
    line, spot = iota((half, nmod), 0), iota((half, nmod), 1)
    owner = line // tok
    same = spot == ((owner // 2) ^ chip) * tok + line % tok
    values = matmul(onehot(same & (owner % 2 == core)), val_ref[...])
    values += matmul(onehot(same & (owner % 2 != core)), other_ref[:, cols:])
    val_out[...] = values.astype(bf16)


def proj_kernel(val_ref, res_ref, out_ref):
    out_ref[...] = matmul(val_ref[...], res_ref[...], (((0,), (0,)), ((), ()))).astype(out_ref.dtype)


def output_kernel(tok, nvoc, cols, *refs):
    f32, bf16 = jnp.float32, jnp.bfloat16
    parts, mains = refs[:nvoc], refs[nvoc : nvoc + 2]
    trunk_ref, res_ref, gain_ref, attn_ref = refs[nvoc + 2 :]
    count, heads, size = attn_ref.shape
    hdim = heads * size
    fold = count // tok
    strip = cols // fold
    voc = lax.axis_index("vocab")
    values = [p[...].astype(f32) for p in parts]
    for k, part in enumerate(values):
        for f in range(fold):
            at = pl.ds(pl.multiple_of((voc ^ k) * cols + f * strip, 128), strip)
            res_ref[:, at] = part[f * tok : (f + 1) * tok, :strip].astype(bf16)
        gains = part[:, strip + hdim : strip + 2 * hdim] + part[:, strip + 2 * hdim :]
        for i in range(cols // hdim):
            at = pl.ds(pl.multiple_of((voc ^ k) * cols + i * hdim, 128), hdim)
            gain_ref[:, at] = gains[i : i + 1]
    total = tree_sum([v[:, strip : strip + hdim] for v in values])
    for i in range(count):
        attn_ref[i] = jnp.concatenate(
            [total[i : i + 1, h * size : (h + 1) * size] for h in range(heads)], axis=0
        ).astype(bf16)
    for c in chunks(trunk_ref.shape[1]):
        trunk_ref[:, c] = tree_sum([m[:, c].astype(f32) for m in mains]).astype(bf16)


def local(
    trunk_hidden,
    mtp_state,
    mtp_gain,
    head_weight,
    target_ids,
    mtp_target_ids,
    attn_values,
    out_proj,
):
    f32, bf16 = jnp.float32, jnp.bfloat16
    tok, width = trunk_hidden.shape
    nrow = lax.axis_size("rows")
    nvoc = lax.axis_size("vocab")
    nchip = nrow // 2
    vrows = head_weight.shape[0]
    hdim, cols = out_proj.shape
    _, size = attn_values.shape[1:]
    ntok = nrow * tok
    nmod = nchip * tok
    tok_voc = ntok // nvoc
    part = functools.partial

    stacked = jnp.concatenate([trunk_hidden, mtp_state], axis=0)
    blocks = swaps([stacked] * nchip, "rows", 2)
    weight_near = swap(head_weight, "rows", 1)
    weight, gain, targets = kernel_call(
        part(prepare_kernel, tok),
        [((vrows, width), bf16), ((1, width), f32), ((1, ntok), jnp.int32)],
        head_weight,
        mtp_gain.reshape(width // 128, 128),
        target_ids.reshape(1, ntok),
        mtp_target_ids.reshape(1, ntok),
    )
    raw, hidden, logits, inverse, stats = kernel_call(
        part(head_kernel, tok, nchip),
        [
            ((ntok, width), bf16),
            ((ntok, width), bf16),
            ((2 * vrows, ntok), f32),
            ((ntok, 1), f32),
            ((nrow * nvoc, 4 * ntok), f32),
        ],
        *blocks,
        weight,
        weight_near,
        gain,
        targets,
    )
    raw_near = swap(raw, "rows", 1)
    everyone = lax.all_to_all(
        stats, ("vocab", "rows"), split_axis=0, concat_axis=0, tiled=True
    )
    grads, grads_away, dot_mean, *pieces = kernel_call(
        part(loss_kernel, tok, nvoc),
        [((vrows, ntok), bf16)] * 2
        + [((ntok, 1), f32)]
        + [((nmod, cols), bf16)] * nvoc
        + [((tok, width), bf16)] * nchip,
        everyone,
        logits,
        targets,
        weight,
        weight_near,
    )
    column, main = pieces[:nvoc], pieces[nvoc:]
    column = swaps(column, "vocab", 1)
    main = swaps(main, "rows", 2)
    grads_near = swap(grads_away, "rows", 1)
    hidden, logit_grads, inverse_near = kernel_call(
        part(rest_kernel, tok),
        [((2 * ntok, width), bf16), ((vrows, 2 * ntok), bf16), ((ntok, 1), f32)],
        raw_near,
        gain,
        hidden,
        grads,
        grads_near,
    )
    grad_head = lax.dot_general(
        logit_grads, hidden, (((1,), (0,)), ((), ())), preferred_element_type=f32
    ).astype(bf16)
    plane = kernel_call(
        part(column_kernel, nvoc),
        [((nmod, cols + size), bf16)] * nchip,
        attn_values,
        *column,
    )
    plane = swaps(plane, "rows", 2)
    (main,) = kernel_call(main_kernel, [((tok, width), bf16)], *main)
    near = swap(main, "vocab", 1)
    module, own_values = kernel_call(
        part(plane_kernel, tok, nchip),
        [((nmod, cols + hdim), bf16), ((nmod, hdim), bf16)],
        grad_head,
        *plane,
        away=(0,),
    )
    (main,) = kernel_call(main_kernel, [((tok, width), bf16)], main, near)
    main = [main, swap(main, "vocab", 2)]
    other = swap(module, "rows", 1)
    residual, values, *parcels = kernel_call(
        part(last_kernel, tok),
        [((ntok, cols), bf16), ((ntok, hdim), bf16)]
        + [((tok_voc, cols * tok // tok_voc + 3 * hdim), bf16)] * nvoc,
        raw,
        raw_near,
        inverse,
        inverse_near,
        dot_mean,
        gain,
        out_proj,
        module,
        other,
        own_values,
        side=[pltpu.VMEM((ntok, hdim), f32)],
    )
    parcels = swaps(parcels, "vocab", 1)
    (grad_out_proj,) = kernel_call(proj_kernel, [((hdim, cols), bf16)], values, residual)
    grad_trunk, grad_residual, grad_gain, grad_attn = kernel_call(
        part(output_kernel, tok, nvoc, cols),
        [
            ((tok, width), bf16),
            ((tok, width), bf16),
            ((1, width), f32),
            ((tok_voc, hdim // size, size), bf16),
        ],
        *parcels,
        *main,
    )
    return (
        grad_trunk,
        grad_residual,
        grad_gain.reshape(width),
        grad_head,
        grad_attn,
        grad_out_proj,
    )


def swaps(parts, axis, unit):
    got = [parts[0]]
    for k in range(1, len(parts)):
        got.append(swap(parts[k], axis, k * unit))
    return got


def choose(*args):
    tok, cols, hdim = args[0].shape[0], args[7].shape[1], args[7].shape[0]
    ntok = lax.axis_size("rows") * tok
    tok_voc = ntok // lax.axis_size("vocab")
    fits = (
        lax.axis_size("rows") == 8
        and ntok == 32
        and         tok_voc == 8
        and lax.axis_size("vocab") == 4
        and tok_voc % tok == 0
        and cols % (128 * tok_voc // tok) == 0
        and hdim % 128 == 0
        and cols % hdim == 0
        and cols // hdim <= tok_voc
        and args[6].shape[1] // (lax.axis_size("rows") // 2) == tok
    )
    if not fits:
        return plain(*args)
    return local(*args)


def solution(mesh):
    return jax.shard_map(
        choose,
        mesh=mesh,
        in_specs=(
            P("rows", None),
            P("rows", None),
            P(),
            P(("vocab", "rows"), None),
            P(),
            P(),
            P("rows", None, None),
            P("rows", "vocab"),
        ),
        out_specs=(
            P("rows", None),
            P("rows", None),
            P(),
            P(("vocab", "rows"), None),
            P("vocab", "rows", None),
            P("rows", "vocab"),
        ),
        check_vma=False,
    )
```

profile of v0, /device:TPU:0, one launch (start us, length us, event | category | flops | bytes accessed | tf_op | source)
XLA Modules:
  0.0 56.6 jit_solution(15157737486109118388)
XLA Ops:
  1.2 0.9 %pad_maximum_fusion.refs_0_ = bf16[8,7168]{1,0:T(8,128)(2,1)S(1)} fusion(bf16[4,7168]{1,0:T(4,128)(2,1)} %param.9, bf16[4,7168]{1,0:T(4,128)(2,1)} %param.8), kind=kLoop, calls=%fused_computation.1 | loop fusion | flops 229376 | bytes 229376 | tf_op jit(solution)/shard_map/concatenate | solution.py:519
  2.1 3.5 %collective-permute-start.2 = (bf16[8,7168]{1,0:T(8,128)(2,1)S(1)}, bf16[8,7168]{1,0:T(8,128)(2,1)S(1)}, u32[]{:S(2)}, u32[]{:S(2)}) collective-permute-start(bf16[8,7168]{1,0:T(8,128)(2,1)S(1)} %pad_maximum_fusion.refs_0_), channel_id=1, source_target_pairs={{0,6},{1,7},{2,4},{3,5},{4,2},{5,3},{6,0},{7,1},{8,14},{9,15},{10,... | collective-permute-start | bytes 344072 | tf_op jit(solution)/shard_map/ppermute | solution.py:17
  6.3 1.6 %copy-done.1 = bf16[144,7168]{1,0:T(8,128)(2,1)S(1)} copy-done((bf16[144,7168]{1,0:T(8,128)(2,1)S(1)}, bf16[144,7168]{1,0:T(8,128)(2,1)}, u32[]{:S(2)}) %copy-start.1) | copy-done | bytes 2064408
  7.8 0.7 %copy-done.4 = bf16[7168]{0:T(1024)(128)(2,1)S(1)} copy-done((bf16[7168]{0:T(1024)(128)(2,1)S(1)}, bf16[7168]{0:T(1024)(128)(2,1)}, u32[]{:S(2)}) %copy-start.4) | copy-done | bytes 14360
  10.0 1.8 %collective-permute-done.1.refs_2_ = bf16[8,7168]{1,0:T(8,128)(2,1)S(1)} collective-permute-done((bf16[8,7168]{1,0:T(8,128)(2,1)S(1)}, bf16[8,7168]{1,0:T(8,128)(2,1)S(1)}, u32[]{:S(2)}, u32[]{:S(2)}) %collective-permute-start.1) | collective-permute-done | bytes 114720 | tf_op jit(solution)/shard_map/ppermute | solution.py:17
  12.2 1.6 %shard_map.128 = (bf16[32,7168]{1,0:T(8,128)(2,1)S(1)}, bf16[32,7168]{1,0:T(8,128)(2,1)S(1)}, f32[288,32]{1,0:T(8,128)S(1)}, f32[32,1]{1,0:T(8,128)S(1)}, f32[32,128]{1,0:T(8,128)S(1)}) custom-call(bf16[8,7168]{1,0:T(8,128)(2,1)S(1)} %pad_maximum_fusion.refs_0_, bf16[8,7168]{1,0:T(8,128)(2,1)S(1)} %collective-permute-done.refs_1_, ...), custom_call_target="tpu_custom_call" | custom-call | tf_op jit(solution)/shard_map/pallas_call | solution.py:204
  13.8 12.2 %all_to_all.11 = f32[32,1,128]{2,1,0:T(1,128)S(1)} all-to-all(f32[32,1,128]{2,1,0:T(1,128)S(1)} %bitcast.11), channel_id=1, replica_groups=mesh['vocab'=4,'rows'=8] {'vocab','rows'}, dimensions={0} | all-to-all | bytes 32768 | tf_op jit(solution)/shard_map/all_to_all | solution.py:546
  25.9 0.9 %shard_map.129 = (bf16[144,32]{1,0:T(8,128)(2,1)S(1)}, bf16[144,32]{1,0:T(8,128)(2,1)S(1)}, f32[32,1]{1,0:T(8,128)S(1)}, bf16[16,1792]{1,0:T(8,128)(2,1)S(1)}, b...) custom-call(f32[32,128]{1,0:T(8,128)S(1)} %bitcast.10, ...), custom_call_target="tpu_custom_call" | custom-call | tf_op jit(solution)/shard_map/pallas_call | solution.py:204
  28.1 2.3 %collective-permute-start.18 = (bf16[4,7168]{1,0:T(4,128)(2,1)S(1)}, bf16[4,7168]{1,0:T(4,128)(2,1)S(1)}, u32[]{:S(2)}, u32[]{:S(2)}) collective-permute-start(bf16[4,7168]{1,0:T(4,128)(2,1)S(1)} %get-tuple-element.75), channel_id=1, source_target_pairs={{0,6},{1,7},{2,4},{3,5},{4,2},{5,3},{6,0},{7,1},{8,14},{9,15},{10,... | collective-permute-start | bytes 172040 | tf_op jit(solution)/shard_map/ppermute | solution.py:17
  32.2 2.7 %collective-permute-start.8 = (bf16[16,1792]{1,0:T(8,128)(2,1)S(1)}, bf16[16,1792]{1,0:T(8,128)(2,1)S(1)}, u32[]{:S(2)}, u32[]{:S(2)}) collective-permute-start(bf16[16,1792]{1,0:T(8,128)(2,1)S(1)} %get-tuple-element.61), channel_id=1, source_target_pairs={{0,24},{8,16},{16,8},{24,0},{1,25},{9,17},{17,9},{25,1},{2,26},{10... | collective-permute-start | bytes 172040 | tf_op jit(solution)/shard_map/ppermute | solution.py:17
  35.2 1.9 %collective-permute-done.7.refs_2_ = bf16[16,1792]{1,0:T(8,128)(2,1)S(1)} collective-permute-done((bf16[16,1792]{1,0:T(8,128)(2,1)S(1)}, bf16[16,1792]{1,0:T(8,128)(2,1)S(1)}, u32[]{:S(2)}, u32[]{:S(2)}) %collective-permute-start.7) | collective-permute-done | bytes 57376 | tf_op jit(solution)/shard_map/ppermute | solution.py:17
  37.1 1.7 %collective-permute-done.8.refs_3_ = bf16[16,1792]{1,0:T(8,128)(2,1)S(1)} collective-permute-done((bf16[16,1792]{1,0:T(8,128)(2,1)S(1)}, bf16[16,1792]{1,0:T(8,128)(2,1)S(1)}, u32[]{:S(2)}, u32[]{:S(2)}) %collective-permute-start.8) | collective-permute-done | bytes 57376 | tf_op jit(solution)/shard_map/ppermute | solution.py:17
  39.0 1.4 %collective-permute-start.9 = (bf16[16,1920]{1,0:T(8,128)(2,1)S(1)}, bf16[16,1920]{1,0:T(8,128)(2,1)S(1)}, u32[]{:S(2)}, u32[]{:S(2)}) collective-permute-start(bf16[16,1920]{1,0:T(8,128)(2,1)S(1)} %get-tuple-element.63), channel_id=1, source_target_pairs={{0,2},{1,3},{2,0},{3,1},{4,6},{5,7},{6,4},{7,5},{8,10},{9,11},{10,... | collective-permute-start | bytes 184328 | tf_op jit(solution)/shard_map/ppermute | solution.py:17
  40.4 2.1 %collective-permute-start.11 = (bf16[16,1920]{1,0:T(8,128)(2,1)S(1)}, bf16[16,1920]{1,0:T(8,128)(2,1)S(1)}, u32[]{:S(2)}, u32[]{:S(2)}) collective-permute-start(bf16[16,1920]{1,0:T(8,128)(2,1)S(1)} %get-tuple-element.65), channel_id=1, source_target_pairs={{0,6},{1,7},{2,4},{3,5},{4,2},{5,3},{6,0},{7,1},{8,14},{9,15},{10,... | collective-permute-start | bytes 184328 | tf_op jit(solution)/shard_map/ppermute | solution.py:17
  43.6 1.0 %collective-permute-done.10.refs_2_ = bf16[16,1920]{1,0:T(8,128)(2,1)S(1)} collective-permute-done((bf16[16,1920]{1,0:T(8,128)(2,1)S(1)}, bf16[16,1920]{1,0:T(8,128)(2,1)S(1)}, u32[]{:S(2)}, u32[]{:S(2)}) %collective-permute-start.10) | collective-permute-done | bytes 61472 | tf_op jit(solution)/shard_map/ppermute | solution.py:17
  44.6 0.9 %collective-permute-done.11.refs_3_ = bf16[16,1920]{1,0:T(8,128)(2,1)S(1)} collective-permute-done((bf16[16,1920]{1,0:T(8,128)(2,1)S(1)}, bf16[16,1920]{1,0:T(8,128)(2,1)S(1)}, u32[]{:S(2)}, u32[]{:S(2)}) %collective-permute-start.11) | collective-permute-done | bytes 61472 | tf_op jit(solution)/shard_map/ppermute | solution.py:17
  45.8 1.1 %collective-permute-done.12.other_ref = bf16[16,2048]{1,0:T(8,128)(2,1)S(1)} collective-permute-done((bf16[16,2048]{1,0:T(8,128)(2,1)S(1)}, bf16[16,2048]{1,0:T(8,128)(2,1)S(1)}, u32[]{:S(2)}, u32[]{:S(2)}) %collective-permute-start.12) | collective-permute-done | bytes 65568 | tf_op jit(solution)/shard_map/ppermute | solution.py:17
  47.6 1.6 %collective-permute-start.13 = (bf16[8,1664]{1,0:T(8,128)(2,1)S(1)}, bf16[8,1664]{1,0:T(8,128)(2,1)S(1)}, u32[]{:S(2)}, u32[]{:S(2)}) collective-permute-start(bf16[8,1664]{1,0:T(8,128)(2,1)S(1)} %get-tuple-element.69), channel_id=1, source_target_pairs={{0,8},{8,0},{16,24},{24,16},{1,9},{9,1},{17,25},{25,17},{2,10},{10... | collective-permute-start | bytes 79880 | tf_op jit(solution)/shard_map/ppermute | solution.py:17
  49.2 1.1 %collective-permute-start.14 = (bf16[8,1664]{1,0:T(8,128)(2,1)S(1)}, bf16[8,1664]{1,0:T(8,128)(2,1)S(1)}, u32[]{:S(2)}, u32[]{:S(2)}) collective-permute-start(bf16[8,1664]{1,0:T(8,128)(2,1)S(1)} %get-tuple-element.70), channel_id=1, source_target_pairs={{0,16},{8,24},{16,0},{24,8},{1,17},{9,25},{17,1},{25,9},{2,18},{10... | collective-permute-start | bytes 79880 | tf_op jit(solution)/shard_map/ppermute | solution.py:17
  50.3 1.7 %collective-permute-start.15 = (bf16[8,1664]{1,0:T(8,128)(2,1)S(1)}, bf16[8,1664]{1,0:T(8,128)(2,1)S(1)}, u32[]{:S(2)}, u32[]{:S(2)}) collective-permute-start(bf16[8,1664]{1,0:T(8,128)(2,1)S(1)} %get-tuple-element.71), channel_id=1, source_target_pairs={{0,24},{8,16},{16,8},{24,0},{1,25},{9,17},{17,9},{25,1},{2,26},{10... | collective-permute-start | bytes 79880 | tf_op jit(solution)/shard_map/ppermute | solution.py:17
  52.0 1.3 %shard_map.137 = bf16[256,1792]{1,0:T(8,128)(2,1)} custom-call(bf16[32,256]{1,0:T(8,128)(2,1)S(1)} %get-tuple-element.80.val_ref, bf16[32,1792]{1,0:T(8,128)(2,1)S(1)} %get-tuple-element.81.res_ref), custom_call_target="tpu_custom_call" | custom-call | tf_op jit(solution)/shard_map/pallas_call | solution.py:204
  53.4 0.8 %collective-permute-done.14.refs_2_ = bf16[8,1664]{1,0:T(8,128)(2,1)S(1)} collective-permute-done((bf16[8,1664]{1,0:T(8,128)(2,1)S(1)}, bf16[8,1664]{1,0:T(8,128)(2,1)S(1)}, u32[]{:S(2)}, u32[]{:S(2)}) %collective-permute-start.14) | collective-permute-done | bytes 26656 | tf_op jit(solution)/shard_map/ppermute | solution.py:17
  54.1 1.8 %collective-permute-done.15.refs_3_ = bf16[8,1664]{1,0:T(8,128)(2,1)S(1)} collective-permute-done((bf16[8,1664]{1,0:T(8,128)(2,1)S(1)}, bf16[8,1664]{1,0:T(8,128)(2,1)S(1)}, u32[]{:S(2)}, u32[]{:S(2)}) %collective-permute-start.15) | collective-permute-done | bytes 26656 | tf_op jit(solution)/shard_map/ppermute | solution.py:17
  55.9 0.7 %shard_map.136 = (bf16[4,7168]{1,0:T(4,128)(2,1)}, bf16[4,7168]{1,0:T(4,128)(2,1)}, f32[1,7168]{1,0:T(1,128)}, bf16[8,2,128]{2,1,0:T(2,128)(2,1)}) custom-call(bf16[8,1664]{1,0:T(8,128)(2,1)S(1)} %get-tuple-element.68.refs_0_, bf16[8,1664]{1,0:T(8,128)(2,1)S(1)} %collective-permute-done.13.refs_1_, bf16[8,1664]{1,0:T(8,128)(2,1)S(1)} %collective-permute-done.14.refs_2_, ...), custom_call_target="tpu_custom_call" | custom-call | tf_op jit(solution)/shard_map/pallas_call | solution.py:204
  (46 shorter events, 8.3 us)
Async XLA Ops:
  0.6 11.5 %collective-permute-start.3 = (bf16[144,7168]{1,0:T(8,128)(2,1)}, bf16[144,7168]{1,0:T(8,128)(2,1)S(1)}, u32[]{:S(2)}, u32[]{:S(2)}) collective-permute-start(bf16[144,7168]{1,0:T(8,128)(2,1)} %w_src.1), channel_id=1, source_target_pairs={{0,1},{1,0},{2,3},{3,2},{4,5},{5,4},{6,7},{7,6},{8,9},{9,8},{10,11... | collective-permute-start | bytes 6193160 | tf_op jit(solution)/shard_map/ppermute | solution.py:17
  2.1 7.9 %collective-permute-start.2 = (bf16[8,7168]{1,0:T(8,128)(2,1)S(1)}, bf16[8,7168]{1,0:T(8,128)(2,1)S(1)}, u32[]{:S(2)}, u32[]{:S(2)}) collective-permute-start(bf16[8,7168]{1,0:T(8,128)(2,1)S(1)} %pad_maximum_fusion.refs_0_), channel_id=1, source_target_pairs={{0,6},{1,7},{2,4},{3,5},{4,2},{5,3},{6,0},{7,1},{8,14},{9,15},{10,... | collective-permute-start | bytes 344072 | tf_op jit(solution)/shard_map/ppermute | solution.py:17
  5.6 6.3 %collective-permute-start.1 = (bf16[8,7168]{1,0:T(8,128)(2,1)S(1)}, bf16[8,7168]{1,0:T(8,128)(2,1)S(1)}, u32[]{:S(2)}, u32[]{:S(2)}) collective-permute-start(bf16[8,7168]{1,0:T(8,128)(2,1)S(1)} %pad_maximum_fusion.refs_0_), channel_id=1, source_target_pairs={{0,4},{1,5},{2,6},{3,7},{4,0},{5,1},{6,2},{7,3},{8,12},{9,13},{10,... | collective-permute-start | bytes 344072 | tf_op jit(solution)/shard_map/ppermute | solution.py:17
  6.1 6.0 %collective-permute-start = (bf16[8,7168]{1,0:T(8,128)(2,1)S(1)}, bf16[8,7168]{1,0:T(8,128)(2,1)S(1)}, u32[]{:S(2)}, u32[]{:S(2)}) collective-permute-start(bf16[8,7168]{1,0:T(8,128)(2,1)S(1)} %pad_maximum_fusion.refs_0_), channel_id=1, source_target_pairs={{0,2},{1,3},{2,0},{3,1},{4,6},{5,7},{6,4},{7,5},{8,10},{9,11},{10,... | collective-permute-start | bytes 344072 | tf_op jit(solution)/shard_map/ppermute | solution.py:17
  13.8 28.8 %collective-permute-start.4 = (bf16[32,7168]{1,0:T(8,128)(2,1)S(1)}, bf16[32,7168]{1,0:T(8,128)(2,1)S(1)}, u32[]{:S(2)}, u32[]{:S(2)}) collective-permute-start(bf16[32,7168]{1,0:T(8,128)(2,1)S(1)} %get-tuple-element.47.raw_ref), channel_id=1, source_target_pairs={{0,1},{1,0},{2,3},{3,2},{4,5},{5,4},{6,7},{7,6},{8,9},{9,8},{10,11... | collective-permute-start | bytes 1376264 | tf_op jit(solution)/shard_map/ppermute | solution.py:17
  25.9 12.9 %copy-start.3 = (bf16[4,16,128]{2,1,0:T(8,128)(2,1)S(1)}, bf16[4,16,128]{2,1,0:T(8,128)(2,1)}, u32[]{:S(2)}) copy-start(bf16[4,16,128]{2,1,0:T(8,128)(2,1)} %attn_ref.1) | copy-start | bytes 49156
  26.9 4.5 %collective-permute-start.16 = (bf16[4,7168]{1,0:T(4,128)(2,1)S(1)}, bf16[4,7168]{1,0:T(4,128)(2,1)S(1)}, u32[]{:S(2)}, u32[]{:S(2)}) collective-permute-start(bf16[4,7168]{1,0:T(4,128)(2,1)S(1)} %get-tuple-element.73), channel_id=1, source_target_pairs={{0,2},{1,3},{2,0},{3,1},{4,6},{5,7},{6,4},{7,5},{8,10},{9,11},{10,... | collective-permute-start | bytes 172040 | tf_op jit(solution)/shard_map/ppermute | solution.py:17
  27.5 4.7 %collective-permute-start.17 = (bf16[4,7168]{1,0:T(4,128)(2,1)S(1)}, bf16[4,7168]{1,0:T(4,128)(2,1)S(1)}, u32[]{:S(2)}, u32[]{:S(2)}) collective-permute-start(bf16[4,7168]{1,0:T(4,128)(2,1)S(1)} %get-tuple-element.74), channel_id=1, source_target_pairs={{0,4},{1,5},{2,6},{3,7},{4,0},{5,1},{6,2},{7,3},{8,12},{9,13},{10,... | collective-permute-start | bytes 172040 | tf_op jit(solution)/shard_map/ppermute | solution.py:17
  28.1 6.7 %collective-permute-start.18 = (bf16[4,7168]{1,0:T(4,128)(2,1)S(1)}, bf16[4,7168]{1,0:T(4,128)(2,1)S(1)}, u32[]{:S(2)}, u32[]{:S(2)}) collective-permute-start(bf16[4,7168]{1,0:T(4,128)(2,1)S(1)} %get-tuple-element.75), channel_id=1, source_target_pairs={{0,6},{1,7},{2,4},{3,5},{4,2},{5,3},{6,0},{7,1},{8,14},{9,15},{10,... | collective-permute-start | bytes 172040 | tf_op jit(solution)/shard_map/ppermute | solution.py:17
  30.4 4.5 %collective-permute-start.6 = (bf16[16,1792]{1,0:T(8,128)(2,1)S(1)}, bf16[16,1792]{1,0:T(8,128)(2,1)S(1)}, u32[]{:S(2)}, u32[]{:S(2)}) collective-permute-start(bf16[16,1792]{1,0:T(8,128)(2,1)S(1)} %get-tuple-element.59), channel_id=1, source_target_pairs={{0,8},{8,0},{16,24},{24,16},{1,9},{9,1},{17,25},{25,17},{2,10},{10... | collective-permute-start | bytes 172040 | tf_op jit(solution)/shard_map/ppermute | solution.py:17
  31.4 5.7 %collective-permute-start.7 = (bf16[16,1792]{1,0:T(8,128)(2,1)S(1)}, bf16[16,1792]{1,0:T(8,128)(2,1)S(1)}, u32[]{:S(2)}, u32[]{:S(2)}) collective-permute-start(bf16[16,1792]{1,0:T(8,128)(2,1)S(1)} %get-tuple-element.60), channel_id=1, source_target_pairs={{0,16},{8,24},{16,0},{24,8},{1,17},{9,25},{17,1},{25,9},{2,18},{10... | collective-permute-start | bytes 172040 | tf_op jit(solution)/shard_map/ppermute | solution.py:17
  32.2 6.6 %collective-permute-start.8 = (bf16[16,1792]{1,0:T(8,128)(2,1)S(1)}, bf16[16,1792]{1,0:T(8,128)(2,1)S(1)}, u32[]{:S(2)}, u32[]{:S(2)}) collective-permute-start(bf16[16,1792]{1,0:T(8,128)(2,1)S(1)} %get-tuple-element.61), channel_id=1, source_target_pairs={{0,24},{8,16},{16,8},{24,0},{1,25},{9,17},{17,9},{25,1},{2,26},{10... | collective-permute-start | bytes 172040 | tf_op jit(solution)/shard_map/ppermute | solution.py:17
  34.8 5.6 %collective-permute-start.5 = (bf16[144,32]{1,0:T(8,128)(2,1)S(1)}, bf16[144,32]{1,0:T(8,128)(2,1)S(1)}, u32[]{:S(2)}, u32[]{:S(2)}) collective-permute-start(bf16[144,32]{1,0:T(8,128)(2,1)S(1)} %get-tuple-element.53), channel_id=1, source_target_pairs={{0,1},{1,0},{2,3},{3,2},{4,5},{5,4},{6,7},{7,6},{8,9},{9,8},{10,11... | collective-permute-start | bytes 27656 | tf_op jit(solution)/shard_map/ppermute | solution.py:17
  34.9 10.8 %collective-permute-start.19 = (bf16[4,7168]{1,0:T(4,128)(2,1)S(1)}, bf16[4,7168]{1,0:T(4,128)(2,1)S(1)}, u32[]{:S(2)}, u32[]{:S(2)}) collective-permute-start(bf16[4,7168]{1,0:T(4,128)(2,1)S(1)} %shard_map.134.refs_0_), channel_id=1, source_target_pairs={{0,8},{8,0},{16,24},{24,16},{1,9},{9,1},{17,25},{25,17},{2,10},{10... | collective-permute-start | bytes 172040 | tf_op jit(solution)/shard_map/ppermute | solution.py:17
  39.0 4.6 %collective-permute-start.9 = (bf16[16,1920]{1,0:T(8,128)(2,1)S(1)}, bf16[16,1920]{1,0:T(8,128)(2,1)S(1)}, u32[]{:S(2)}, u32[]{:S(2)}) collective-permute-start(bf16[16,1920]{1,0:T(8,128)(2,1)S(1)} %get-tuple-element.63), channel_id=1, source_target_pairs={{0,2},{1,3},{2,0},{3,1},{4,6},{5,7},{6,4},{7,5},{8,10},{9,11},{10,... | collective-permute-start | bytes 184328 | tf_op jit(solution)/shard_map/ppermute | solution.py:17
  40.4 4.2 %collective-permute-start.10 = (bf16[16,1920]{1,0:T(8,128)(2,1)S(1)}, bf16[16,1920]{1,0:T(8,128)(2,1)S(1)}, u32[]{:S(2)}, u32[]{:S(2)}) collective-permute-start(bf16[16,1920]{1,0:T(8,128)(2,1)S(1)} %get-tuple-element.64), channel_id=1, source_target_pairs={{0,4},{1,5},{2,6},{3,7},{4,0},{5,1},{6,2},{7,3},{8,12},{9,13},{10,... | collective-permute-start | bytes 184328 | tf_op jit(solution)/shard_map/ppermute | solution.py:17
  40.4 5.1 %collective-permute-start.11 = (bf16[16,1920]{1,0:T(8,128)(2,1)S(1)}, bf16[16,1920]{1,0:T(8,128)(2,1)S(1)}, u32[]{:S(2)}, u32[]{:S(2)}) collective-permute-start(bf16[16,1920]{1,0:T(8,128)(2,1)S(1)} %get-tuple-element.65), channel_id=1, source_target_pairs={{0,6},{1,7},{2,4},{3,5},{4,2},{5,3},{6,0},{7,1},{8,14},{9,15},{10,... | collective-permute-start | bytes 184328 | tf_op jit(solution)/shard_map/ppermute | solution.py:17
  42.8 4.1 %copy-start.2 = (bf16[256,1792]{1,0:T(8,128)(2,1)S(1)}, bf16[256,1792]{1,0:T(8,128)(2,1)}, u32[]{:S(2)}) copy-start(bf16[256,1792]{1,0:T(8,128)(2,1)} %proj_ref.1) | copy-start | bytes 2752516
  43.5 4.0 %copy-start = (bf16[144,7168]{1,0:T(8,128)(2,1)}, bf16[144,7168]{1,0:T(8,128)(2,1)S(1)}, u32[]{:S(2)}) copy-start(bf16[144,7168]{1,0:T(8,128)(2,1)S(1)} %convolution_convert_fusion.hold_ref) | copy-start | bytes 6193156
  45.7 1.3 %collective-permute-start.12 = (bf16[16,2048]{1,0:T(8,128)(2,1)S(1)}, bf16[16,2048]{1,0:T(8,128)(2,1)S(1)}, u32[]{:S(2)}, u32[]{:S(2)}) collective-permute-start(bf16[16,2048]{1,0:T(8,128)(2,1)S(1)} %get-tuple-element.66.own_ref), channel_id=1, source_target_pairs={{0,1},{1,0},{2,3},{3,2},{4,5},{5,4},{6,7},{7,6},{8,9},{9,8},{10,11... | collective-permute-start | bytes 196616 | tf_op jit(solution)/shard_map/ppermute | solution.py:17
  45.7 7.6 %collective-permute-start.20 = (bf16[4,7168]{1,0:T(4,128)(2,1)S(1)}, bf16[4,7168]{1,0:T(4,128)(2,1)S(1)}, u32[]{:S(2)}, u32[]{:S(2)}) collective-permute-start(bf16[4,7168]{1,0:T(4,128)(2,1)S(1)} %shard_map.135.refs_4_), channel_id=1, source_target_pairs={{0,16},{8,24},{16,0},{24,8},{1,17},{9,25},{17,1},{25,9},{2,18},{10... | collective-permute-start | bytes 172040 | tf_op jit(solution)/shard_map/ppermute | solution.py:17
  47.6 5.8 %collective-permute-start.13 = (bf16[8,1664]{1,0:T(8,128)(2,1)S(1)}, bf16[8,1664]{1,0:T(8,128)(2,1)S(1)}, u32[]{:S(2)}, u32[]{:S(2)}) collective-permute-start(bf16[8,1664]{1,0:T(8,128)(2,1)S(1)} %get-tuple-element.69), channel_id=1, source_target_pairs={{0,8},{8,0},{16,24},{24,16},{1,9},{9,1},{17,25},{25,17},{2,10},{10... | collective-permute-start | bytes 79880 | tf_op jit(solution)/shard_map/ppermute | solution.py:17
  49.2 5.0 %collective-permute-start.14 = (bf16[8,1664]{1,0:T(8,128)(2,1)S(1)}, bf16[8,1664]{1,0:T(8,128)(2,1)S(1)}, u32[]{:S(2)}, u32[]{:S(2)}) collective-permute-start(bf16[8,1664]{1,0:T(8,128)(2,1)S(1)} %get-tuple-element.70), channel_id=1, source_target_pairs={{0,16},{8,24},{16,0},{24,8},{1,17},{9,25},{17,1},{25,9},{2,18},{10... | collective-permute-start | bytes 79880 | tf_op jit(solution)/shard_map/ppermute | solution.py:17
  50.3 5.6 %collective-permute-start.15 = (bf16[8,1664]{1,0:T(8,128)(2,1)S(1)}, bf16[8,1664]{1,0:T(8,128)(2,1)S(1)}, u32[]{:S(2)}, u32[]{:S(2)}) collective-permute-start(bf16[8,1664]{1,0:T(8,128)(2,1)S(1)} %get-tuple-element.71), channel_id=1, source_target_pairs={{0,24},{8,16},{16,8},{24,0},{1,25},{9,17},{17,9},{25,1},{2,26},{10... | collective-permute-start | bytes 79880 | tf_op jit(solution)/shard_map/ppermute | solution.py:17
  (4 other events, 3.6 us)
where the time goes:
time: 56.9 us; the launch traced here: 56.6 us
  starting transfers between devices  20.5 us (36%)
  blocking collectives  12.2 us (21%)
  waiting for transfers between devices  11.9 us (21%)
  Pallas kernels  6.04 us (11%)
  local copies, waits for them, and re-layouts  3.62 us (6%)
  other arithmetic  0.91 us (2%)
  between operations  0.78 us (1%)
  matrix products  0.68 us (1%)
    ppermute x21, starting transfers between devices, swap(): return lax.ppermute(x, axis, [(i, i ^ k) for i in range(n)])  20.5 us
    all_to_all x1, blocking collectives, local(): lax.all_to_all(stats, ('vocab', 'rows'), split_axis=0, concat_axis=0, til...  12.2 us
    ppermute x21, waiting for transfers between devices, swap(): return lax.ppermute(x, axis, [(i, i ^ k) for i in range(n)])  11.9 us
    pallas_call x11, Pallas kernels, kernel_call(): pl.pallas_call(body, in_specs=[hbm if k in away else vmem for k in range(...  6.04 us
    unnamed x14, local copies, waits for them, and re-layouts  3.62 us
  transfers between devices with their start and end apart: 21, of which 11 were waited for; matrix products, arithmetic and copies ran while one was open for 3% of the time, Pallas kernels for 7%

commit v1 on v0

--- a/solution.py
+++ b/solution.py
@@ -285,6 +285,12 @@
         other += matmul(part_ref[:, c], h, NT)
     lt = jnp.concatenate([own, other], axis=0)
     lt_ref[...] = lt
+    left, tail = inv_ref[...], jnp.zeros((rows, 128), f32)
+    for k in range(3):
+        term = left.astype(bf16).astype(f32)
+        tail = jnp.where(iota(tail.shape, 1) == k, term, tail)
+        left = left - term
+    raw_ref[:, width:] = tail.astype(bf16)
     peak = jnp.max(lt, axis=0, keepdims=True)
     below = lt - peak
     weight = jnp.exp(below)
@@ -347,12 +353,11 @@
             out[:, at] = total[half + j * tok : half + (j + 1) * tok].astype(bf16)
 
 
-def rest_kernel(tok, raw_ref, gain_ref, hid_ref, own_ref, got_ref, hid_out, gt_out, inv_out):
-    f32, bf16 = jnp.float32, jnp.bfloat16
-    rows, width = raw_ref.shape
+def rest_kernel(tok, raw_ref, gain_ref, hid_ref, own_ref, got_ref, hid_out, gt_out):
+    f32, bf16 = jnp.float32, jnp.bfloat16
+    rows, width = hid_ref.shape
     module = (iota((rows, 1), 0) // tok) % 2 == 1
-    inverse = inverse_of(raw_ref, slice(None))
-    inv_out[...] = inverse
+    inverse = jnp.sum(raw_ref[:, width:].astype(f32), axis=1, keepdims=True)
     for c in chunks(width):
         x = raw_ref[:, c].astype(f32)
         hid_out[:rows, c] = hid_ref[:, c]
@@ -384,7 +389,7 @@
         )
 
 
-def plane_kernel(tok, nchip, hold_ref, *refs):
+def plane_kernel(tok, nchip, *refs):
     f32, bf16 = jnp.float32, jnp.bfloat16
     parts, (swap_ref, val_ref) = refs[:nchip], refs[nchip:]
     nmod, hdim = val_ref.shape
@@ -404,7 +409,7 @@
 
 
 def last_kernel(
-    tok, raw_ref, part_ref, inv_ref, far_ref, dot_ref, gain_ref, proj_ref, own_ref, other_ref, val_ref, res_ref, val_out, *outs
+    tok, raw_ref, part_ref, inv_ref, dot_ref, gain_ref, proj_ref, own_ref, other_ref, val_ref, res_ref, val_out, *outs
 ):
     f32, bf16 = jnp.float32, jnp.bfloat16
     parcels, (scratch,) = outs[:-1], outs[-1:]
@@ -421,7 +426,8 @@
     grad = matmul(onehot(same & (owner % 2 == core)), own_ref[:, :cols])
     grad += matmul(onehot(same & (owner % 2 != core)), other_ref[:, :cols])
     start = pl.multiple_of(voc * cols, 128)
-    near = jnp.concatenate([across(inv_ref[...]), across(far_ref[...])], axis=1)
+    far = jnp.sum(part_ref[:, gain_ref.shape[1] :].astype(f32), axis=1, keepdims=True)
+    near = jnp.concatenate([across(inv_ref[...]), across(far)], axis=1)
     inverse = in_order(near, tok, half)
     at = pl.ds(start, cols)
     state = jnp.concatenate([raw_ref[:, at], part_ref[:, at]], axis=0)
@@ -446,14 +452,12 @@
     pieces = [gain_piece[:, c : c + hdim] for c in range(0, cols, hdim)]
     pieces += [jnp.zeros((1, hdim), f32)] * (tok_voc - len(pieces))
     gains = jnp.concatenate(pieces, axis=0)
-    high = gains.astype(bf16)
-    low = (gains - high.astype(f32)).astype(bf16)
+    gains = gains.astype(bf16)
     for k, out in enumerate(parcels):
         block = scratch[pl.ds(pl.multiple_of((voc ^ k) * tok_voc, tok_voc), tok_voc), :]
         out[:, :strip] = mine
         out[:, strip : strip + hdim] = block.astype(bf16)
-        out[:, strip + hdim : strip + 2 * hdim] = high
-        out[:, strip + 2 * hdim :] = low
+        out[:, strip + hdim :] = gains
     line, spot = iota((half, nmod), 0), iota((half, nmod), 1)
     owner = line // tok
     same = spot == ((owner // 2) ^ chip) * tok + line % tok
@@ -466,7 +470,7 @@
     out_ref[...] = matmul(val_ref[...], res_ref[...], (((0,), (0,)), ((), ()))).astype(out_ref.dtype)
 
 
-def output_kernel(tok, nvoc, cols, *refs):
+def output_kernel(tok, nvoc, cols, hold_ref, *refs):
     f32, bf16 = jnp.float32, jnp.bfloat16
     parts, mains = refs[:nvoc], refs[nvoc : nvoc + 2]
     trunk_ref, res_ref, gain_ref, attn_ref = refs[nvoc + 2 :]
@@ -480,7 +484,7 @@
         for f in range(fold):
             at = pl.ds(pl.multiple_of((voc ^ k) * cols + f * strip, 128), strip)
             res_ref[:, at] = part[f * tok : (f + 1) * tok, :strip].astype(bf16)
-        gains = part[:, strip + hdim : strip + 2 * hdim] + part[:, strip + 2 * hdim :]
+        gains = part[:, strip + hdim :]
         for i in range(cols // hdim):
             at = pl.ds(pl.multiple_of((voc ^ k) * cols + i * hdim, 128), hdim)
             gain_ref[:, at] = gains[i : i + 1]
@@ -530,7 +534,7 @@
     raw, hidden, logits, inverse, stats = kernel_call(
         part(head_kernel, tok, nchip),
         [
-            ((ntok, width), bf16),
+            ((ntok, width + 128), bf16),
             ((ntok, width), bf16),
             ((2 * vrows, ntok), f32),
             ((ntok, 1), f32),
@@ -562,9 +566,9 @@
     column = swaps(column, "vocab", 1)
     main = swaps(main, "rows", 2)
     grads_near = swap(grads_away, "rows", 1)
-    hidden, logit_grads, inverse_near = kernel_call(
+    hidden, logit_grads = kernel_call(
         part(rest_kernel, tok),
-        [((2 * ntok, width), bf16), ((vrows, 2 * ntok), bf16), ((ntok, 1), f32)],
+        [((2 * ntok, width), bf16), ((vrows, 2 * ntok), bf16)],
         raw_near,
         gain,
         hidden,
@@ -586,9 +590,7 @@
     module, own_values = kernel_call(
         part(plane_kernel, tok, nchip),
         [((nmod, cols + hdim), bf16), ((nmod, hdim), bf16)],
-        grad_head,
         *plane,
-        away=(0,),
     )
     (main,) = kernel_call(main_kernel, [((tok, width), bf16)], main, near)
     main = [main, swap(main, "vocab", 2)]
@@ -596,11 +598,10 @@
     residual, values, *parcels = kernel_call(
         part(last_kernel, tok),
         [((ntok, cols), bf16), ((ntok, hdim), bf16)]
-        + [((tok_voc, cols * tok // tok_voc + 3 * hdim), bf16)] * nvoc,
+        + [((tok_voc, cols * tok // tok_voc + 2 * hdim), bf16)] * nvoc,
         raw,
         raw_near,
         inverse,
-        inverse_near,
         dot_mean,
         gain,
         out_proj,
@@ -619,8 +620,10 @@
             ((1, width), f32),
             ((tok_voc, hdim // size, size), bf16),
         ],
+        grad_head,
         *parcels,
         *main,
+        away=(0,),
     )
     return (
         grad_trunk,

time: 56.9 us -> 61.4 us (1.079)
  starting transfers between devices: 20.5 us -> 23.1 us
  waiting for transfers between devices: 11.9 us -> 13.7 us
    ppermute x21, starting transfers between devices: 20.5 us -> 23.1 us  [swap(): return lax.ppermute(x, axis, [(i, i ^ k) for i in range(n)])]
    ppermute x21, waiting for transfers between devices: 11.9 us -> 13.7 us  [swap(): return lax.ppermute(x, axis, [(i, i ^ k) for i in range(n)])]
where the time goes in v1:
time: 61.4 us; the launch traced here: 61.1 us
  starting transfers between devices  23.1 us (38%)
  waiting for transfers between devices  13.7 us (22%)
  blocking collectives  12.1 us (20%)
  Pallas kernels  6.32 us (10%)
  local copies, waits for them, and re-layouts  3.61 us (6%)
  other arithmetic  0.91 us (1%)
  between operations  0.74 us (1%)
  matrix products  0.68 us (1%)
    ppermute x21, starting transfers between devices, swap(): return lax.ppermute(x, axis, [(i, i ^ k) for i in range(n)])  23.1 us
    ppermute x21, waiting for transfers between devices, swap(): return lax.ppermute(x, axis, [(i, i ^ k) for i in range(n)])  13.7 us
    all_to_all x1, blocking collectives, local(): lax.all_to_all(stats, ('vocab', 'rows'), split_axis=0, concat_axis=0, til...  12.1 us
    pallas_call x11, Pallas kernels, kernel_call(): pl.pallas_call(body, in_specs=[hbm if k in away else vmem for k in range(...  6.32 us
    unnamed x14, local copies, waits for them, and re-layouts  3.61 us
  transfers between devices with their start and end apart: 21, of which 11 were waited for; matrix products, arithmetic and copies ran while one was open for 3% of the time, Pallas kernels for 7%

profile of v1, /device:TPU:0, one launch (start us, length us, event | category | flops | bytes accessed | tf_op | source)
XLA Modules:
  0.0 61.1 jit_solution(14629725882130114910)
XLA Ops:
  1.2 0.9 %pad_maximum_fusion.refs_0_ = bf16[8,7168]{1,0:T(8,128)(2,1)S(1)} fusion(bf16[4,7168]{1,0:T(4,128)(2,1)} %param.9, bf16[4,7168]{1,0:T(4,128)(2,1)} %param.8), kind=kLoop, calls=%fused_computation.1 | loop fusion | flops 229376 | bytes 229376 | tf_op jit(solution)/shard_map/concatenate | solution.py:523
  2.1 3.5 %collective-permute-start.2 = (bf16[8,7168]{1,0:T(8,128)(2,1)S(1)}, bf16[8,7168]{1,0:T(8,128)(2,1)S(1)}, u32[]{:S(2)}, u32[]{:S(2)}) collective-permute-start(bf16[8,7168]{1,0:T(8,128)(2,1)S(1)} %pad_maximum_fusion.refs_0_), channel_id=1, source_target_pairs={{0,6},{1,7},{2,4},{3,5},{4,2},{5,3},{6,0},{7,1},{8,14},{9,15},{10,... | collective-permute-start | bytes 344072 | tf_op jit(solution)/shard_map/ppermute | solution.py:17
  6.3 1.6 %copy-done.1 = bf16[144,7168]{1,0:T(8,128)(2,1)S(1)} copy-done((bf16[144,7168]{1,0:T(8,128)(2,1)S(1)}, bf16[144,7168]{1,0:T(8,128)(2,1)}, u32[]{:S(2)}) %copy-start.1) | copy-done | bytes 2064408
  7.8 0.7 %copy-done.4 = bf16[7168]{0:T(1024)(128)(2,1)S(1)} copy-done((bf16[7168]{0:T(1024)(128)(2,1)S(1)}, bf16[7168]{0:T(1024)(128)(2,1)}, u32[]{:S(2)}) %copy-start.4) | copy-done | bytes 14360
  10.0 1.8 %collective-permute-done.1.refs_2_ = bf16[8,7168]{1,0:T(8,128)(2,1)S(1)} collective-permute-done((bf16[8,7168]{1,0:T(8,128)(2,1)S(1)}, bf16[8,7168]{1,0:T(8,128)(2,1)S(1)}, u32[]{:S(2)}, u32[]{:S(2)}) %collective-permute-start.1) | collective-permute-done | bytes 114720 | tf_op jit(solution)/shard_map/ppermute | solution.py:17
  12.2 1.6 %shard_map.128 = (bf16[32,7296]{1,0:T(8,128)(2,1)S(1)}, bf16[32,7168]{1,0:T(8,128)(2,1)S(1)}, f32[288,32]{1,0:T(8,128)S(1)}, f32[32,1]{1,0:T(8,128)S(1)}, f32[32,128]{1,0:T(8,128)S(1)}) custom-call(bf16[8,7168]{1,0:T(8,128)(2,1)S(1)} %pad_maximum_fusion.refs_0_, bf16[8,7168]{1,0:T(8,128)(2,1)S(1)} %collective-permute-done.refs_1_, ...), custom_call_target="tpu_custom_call" | custom-call | tf_op jit(solution)/shard_map/pallas_call | solution.py:204
  13.8 12.1 %all_to_all.11 = f32[32,1,128]{2,1,0:T(1,128)S(1)} all-to-all(f32[32,1,128]{2,1,0:T(1,128)S(1)} %bitcast.11), channel_id=1, replica_groups=mesh['vocab'=4,'rows'=8] {'vocab','rows'}, dimensions={0} | all-to-all | bytes 32768 | tf_op jit(solution)/shard_map/all_to_all | solution.py:550
  26.0 0.9 %shard_map.129 = (bf16[144,32]{1,0:T(8,128)(2,1)S(1)}, bf16[144,32]{1,0:T(8,128)(2,1)S(1)}, f32[32,1]{1,0:T(8,128)S(1)}, bf16[16,1792]{1,0:T(8,128)(2,1)S(1)}, b...) custom-call(f32[32,128]{1,0:T(8,128)S(1)} %bitcast.10, ...), custom_call_target="tpu_custom_call" | custom-call | tf_op jit(solution)/shard_map/pallas_call | solution.py:204
  28.1 3.2 %collective-permute-start.8 = (bf16[16,1792]{1,0:T(8,128)(2,1)S(1)}, bf16[16,1792]{1,0:T(8,128)(2,1)S(1)}, u32[]{:S(2)}, u32[]{:S(2)}) collective-permute-start(bf16[16,1792]{1,0:T(8,128)(2,1)S(1)} %get-tuple-element.59), channel_id=1, source_target_pairs={{0,24},{8,16},{16,8},{24,0},{1,25},{9,17},{17,9},{25,1},{2,26},{10... | collective-permute-start | bytes 172040 | tf_op jit(solution)/shard_map/ppermute | solution.py:17
  31.7 3.1 %collective-permute-done.7.refs_2_ = bf16[16,1792]{1,0:T(8,128)(2,1)S(1)} collective-permute-done((bf16[16,1792]{1,0:T(8,128)(2,1)S(1)}, bf16[16,1792]{1,0:T(8,128)(2,1)S(1)}, u32[]{:S(2)}, u32[]{:S(2)}) %collective-permute-start.7) | collective-permute-done | bytes 57376 | tf_op jit(solution)/shard_map/ppermute | solution.py:17
  35.0 0.7 %collective-permute-start.9 = (bf16[16,1920]{1,0:T(8,128)(2,1)S(1)}, bf16[16,1920]{1,0:T(8,128)(2,1)S(1)}, u32[]{:S(2)}, u32[]{:S(2)}) collective-permute-start(bf16[16,1920]{1,0:T(8,128)(2,1)S(1)} %get-tuple-element.61), channel_id=1, source_target_pairs={{0,2},{1,3},{2,0},{3,1},{4,6},{5,7},{6,4},{7,5},{8,10},{9,11},{10,... | collective-permute-start | bytes 184328 | tf_op jit(solution)/shard_map/ppermute | solution.py:17
  36.3 2.3 %collective-permute-start.11 = (bf16[16,1920]{1,0:T(8,128)(2,1)S(1)}, bf16[16,1920]{1,0:T(8,128)(2,1)S(1)}, u32[]{:S(2)}, u32[]{:S(2)}) collective-permute-start(bf16[16,1920]{1,0:T(8,128)(2,1)S(1)} %get-tuple-element.63), channel_id=1, source_target_pairs={{0,6},{1,7},{2,4},{3,5},{4,2},{5,3},{6,0},{7,1},{8,14},{9,15},{10,... | collective-permute-start | bytes 184328 | tf_op jit(solution)/shard_map/ppermute | solution.py:17
  38.5 0.7 %collective-permute-start.16 = (bf16[4,7168]{1,0:T(4,128)(2,1)S(1)}, bf16[4,7168]{1,0:T(4,128)(2,1)S(1)}, u32[]{:S(2)}, u32[]{:S(2)}) collective-permute-start(bf16[4,7168]{1,0:T(4,128)(2,1)S(1)} %get-tuple-element.71), channel_id=1, source_target_pairs={{0,2},{1,3},{2,0},{3,1},{4,6},{5,7},{6,4},{7,5},{8,10},{9,11},{10,... | collective-permute-start | bytes 172040 | tf_op jit(solution)/shard_map/ppermute | solution.py:17
  40.5 1.5 %collective-permute-start.18 = (bf16[4,7168]{1,0:T(4,128)(2,1)S(1)}, bf16[4,7168]{1,0:T(4,128)(2,1)S(1)}, u32[]{:S(2)}, u32[]{:S(2)}) collective-permute-start(bf16[4,7168]{1,0:T(4,128)(2,1)S(1)} %get-tuple-element.73), channel_id=1, source_target_pairs={{0,6},{1,7},{2,4},{3,5},{4,2},{5,3},{6,0},{7,1},{8,14},{9,15},{10,... | collective-permute-start | bytes 172040 | tf_op jit(solution)/shard_map/ppermute | solution.py:17
  42.7 0.9 %collective-permute-done.17.refs_2_ = bf16[4,7168]{1,0:T(4,128)(2,1)S(1)} collective-permute-done((bf16[4,7168]{1,0:T(4,128)(2,1)S(1)}, bf16[4,7168]{1,0:T(4,128)(2,1)S(1)}, u32[]{:S(2)}, u32[]{:S(2)}) %collective-permute-start.17) | collective-permute-done | bytes 57376 | tf_op jit(solution)/shard_map/ppermute | solution.py:17
  43.6 2.0 %collective-permute-done.18.refs_3_ = bf16[4,7168]{1,0:T(4,128)(2,1)S(1)} collective-permute-done((bf16[4,7168]{1,0:T(4,128)(2,1)S(1)}, bf16[4,7168]{1,0:T(4,128)(2,1)S(1)}, u32[]{:S(2)}, u32[]{:S(2)}) %collective-permute-start.18) | collective-permute-done | bytes 57376 | tf_op jit(solution)/shard_map/ppermute | solution.py:17
  45.7 1.0 %collective-permute-start.19 = (bf16[4,7168]{1,0:T(4,128)(2,1)S(1)}, bf16[4,7168]{1,0:T(4,128)(2,1)S(1)}, u32[]{:S(2)}, u32[]{:S(2)}) collective-permute-start(bf16[4,7168]{1,0:T(4,128)(2,1)S(1)} %shard_map.134.refs_0_), channel_id=1, source_target_pairs={{0,8},{8,0},{16,24},{24,16},{1,9},{9,1},{17,25},{25,17},{2,10},{10... | collective-permute-start | bytes 172040 | tf_op jit(solution)/shard_map/ppermute | solution.py:17
  46.7 3.2 %collective-permute-done.19.refs_1_ = bf16[4,7168]{1,0:T(4,128)(2,1)S(1)} collective-permute-done((bf16[4,7168]{1,0:T(4,128)(2,1)S(1)}, bf16[4,7168]{1,0:T(4,128)(2,1)S(1)}, u32[]{:S(2)}, u32[]{:S(2)}) %collective-permute-start.19) | collective-permute-done | bytes 57376 | tf_op jit(solution)/shard_map/ppermute | solution.py:17
  49.9 2.2 %collective-permute-start.20 = (bf16[4,7168]{1,0:T(4,128)(2,1)S(1)}, bf16[4,7168]{1,0:T(4,128)(2,1)S(1)}, u32[]{:S(2)}, u32[]{:S(2)}) collective-permute-start(bf16[4,7168]{1,0:T(4,128)(2,1)S(1)} %shard_map.135.refs_4_), channel_id=1, source_target_pairs={{0,16},{8,24},{16,0},{24,8},{1,17},{9,25},{17,1},{25,9},{2,18},{10... | collective-permute-start | bytes 172040 | tf_op jit(solution)/shard_map/ppermute | solution.py:17
  52.8 2.0 %collective-permute-start.13 = (bf16[8,1408]{1,0:T(8,128)(2,1)S(1)}, bf16[8,1408]{1,0:T(8,128)(2,1)S(1)}, u32[]{:S(2)}, u32[]{:S(2)}) collective-permute-start(bf16[8,1408]{1,0:T(8,128)(2,1)S(1)} %get-tuple-element.67), channel_id=1, source_target_pairs={{0,8},{8,0},{16,24},{24,16},{1,9},{9,1},{17,25},{25,17},{2,10},{10... | collective-permute-start | bytes 67592 | tf_op jit(solution)/shard_map/ppermute | solution.py:17
  54.8 2.4 %collective-permute-start.15 = (bf16[8,1408]{1,0:T(8,128)(2,1)S(1)}, bf16[8,1408]{1,0:T(8,128)(2,1)S(1)}, u32[]{:S(2)}, u32[]{:S(2)}) collective-permute-start(bf16[8,1408]{1,0:T(8,128)(2,1)S(1)} %get-tuple-element.69), channel_id=1, source_target_pairs={{0,24},{8,16},{16,8},{24,0},{1,25},{9,17},{17,9},{25,1},{2,26},{10... | collective-permute-start | bytes 67592 | tf_op jit(solution)/shard_map/ppermute | solution.py:17
  57.5 0.7 %convolution_convert_fusion.hold_ref = bf16[144,7168]{1,0:T(8,128)(2,1)S(1)} fusion(bf16[144,64]{1,0:T(8,128)(2,1)S(1)} %get-tuple-element.52, bf16[64,7168]{1,0:T(8,128)(2,1)S(1)} %get-tuple-element.53), kind=kOutput, calls=%fused_computation | convolution fusion | flops 133152768 | bytes 3000320 | tf_op jit(solution)/shard_map/dot_general | solution.py:578
  58.2 1.6 %shard_map.137 = bf16[256,1792]{1,0:T(8,128)(2,1)} custom-call(bf16[32,256]{1,0:T(8,128)(2,1)S(1)} %get-tuple-element.78.val_ref, bf16[32,1792]{1,0:T(8,128)(2,1)S(1)} %get-tuple-element.79.res_ref), custom_call_target="tpu_custom_call" | custom-call | tf_op jit(solution)/shard_map/pallas_call | solution.py:204
  60.4 0.7 %shard_map.136 = (bf16[4,7168]{1,0:T(4,128)(2,1)}, bf16[4,7168]{1,0:T(4,128)(2,1)}, f32[1,7168]{1,0:T(1,128)}, bf16[8,2,128]{2,1,0:T(2,128)(2,1)}) custom-call(bf16[144,7168]{1,0:T(8,128)(2,1)S(1)} %convolution_convert_fusion.hold_ref, bf16[8,1408]{1,0:T(8,128)(2,1)S(1)} %get-tuple-element.66.refs_0_, bf16[8,1408]{1,0:T(8,128)(2,1)S(1)} %collective-permute-done.13.refs_1_, ...), custom_call_target="tpu_custom_call" | custom-call | tf_op jit(solution)/shard_map/pallas_call | solution.py:204
  (46 shorter events, 8.9 us)
Async XLA Ops:
  0.6 11.5 %collective-permute-start.3 = (bf16[144,7168]{1,0:T(8,128)(2,1)}, bf16[144,7168]{1,0:T(8,128)(2,1)S(1)}, u32[]{:S(2)}, u32[]{:S(2)}) collective-permute-start(bf16[144,7168]{1,0:T(8,128)(2,1)} %w_src.1), channel_id=1, source_target_pairs={{0,1},{1,0},{2,3},{3,2},{4,5},{5,4},{6,7},{7,6},{8,9},{9,8},{10,11... | collective-permute-start | bytes 6193160 | tf_op jit(solution)/shard_map/ppermute | solution.py:17
  2.1 7.9 %collective-permute-start.2 = (bf16[8,7168]{1,0:T(8,128)(2,1)S(1)}, bf16[8,7168]{1,0:T(8,128)(2,1)S(1)}, u32[]{:S(2)}, u32[]{:S(2)}) collective-permute-start(bf16[8,7168]{1,0:T(8,128)(2,1)S(1)} %pad_maximum_fusion.refs_0_), channel_id=1, source_target_pairs={{0,6},{1,7},{2,4},{3,5},{4,2},{5,3},{6,0},{7,1},{8,14},{9,15},{10,... | collective-permute-start | bytes 344072 | tf_op jit(solution)/shard_map/ppermute | solution.py:17
  5.6 6.3 %collective-permute-start.1 = (bf16[8,7168]{1,0:T(8,128)(2,1)S(1)}, bf16[8,7168]{1,0:T(8,128)(2,1)S(1)}, u32[]{:S(2)}, u32[]{:S(2)}) collective-permute-start(bf16[8,7168]{1,0:T(8,128)(2,1)S(1)} %pad_maximum_fusion.refs_0_), channel_id=1, source_target_pairs={{0,4},{1,5},{2,6},{3,7},{4,0},{5,1},{6,2},{7,3},{8,12},{9,13},{10,... | collective-permute-start | bytes 344072 | tf_op jit(solution)/shard_map/ppermute | solution.py:17
  6.1 6.0 %collective-permute-start = (bf16[8,7168]{1,0:T(8,128)(2,1)S(1)}, bf16[8,7168]{1,0:T(8,128)(2,1)S(1)}, u32[]{:S(2)}, u32[]{:S(2)}) collective-permute-start(bf16[8,7168]{1,0:T(8,128)(2,1)S(1)} %pad_maximum_fusion.refs_0_), channel_id=1, source_target_pairs={{0,2},{1,3},{2,0},{3,1},{4,6},{5,7},{6,4},{7,5},{8,10},{9,11},{10,... | collective-permute-start | bytes 344072 | tf_op jit(solution)/shard_map/ppermute | solution.py:17
  13.8 38.4 %collective-permute-start.4 = (bf16[32,7296]{1,0:T(8,128)(2,1)S(1)}, bf16[32,7296]{1,0:T(8,128)(2,1)S(1)}, u32[]{:S(2)}, u32[]{:S(2)}) collective-permute-start(bf16[32,7296]{1,0:T(8,128)(2,1)S(1)} %get-tuple-element.46.raw_ref), channel_id=1, source_target_pairs={{0,1},{1,0},{2,3},{3,2},{4,5},{5,4},{6,7},{7,6},{8,9},{9,8},{10,11... | collective-permute-start | bytes 1400840 | tf_op jit(solution)/shard_map/ppermute | solution.py:17
  26.0 8.9 %copy-start.3 = (bf16[4,16,128]{2,1,0:T(8,128)(2,1)S(1)}, bf16[4,16,128]{2,1,0:T(8,128)(2,1)}, u32[]{:S(2)}) copy-start(bf16[4,16,128]{2,1,0:T(8,128)(2,1)} %attn_ref.1) | copy-start | bytes 49156
  26.0 26.2 %copy-start.2 = (bf16[256,1792]{1,0:T(8,128)(2,1)S(1)}, bf16[256,1792]{1,0:T(8,128)(2,1)}, u32[]{:S(2)}) copy-start(bf16[256,1792]{1,0:T(8,128)(2,1)} %proj_ref.1) | copy-start | bytes 2752516
  26.9 4.8 %collective-permute-start.6 = (bf16[16,1792]{1,0:T(8,128)(2,1)S(1)}, bf16[16,1792]{1,0:T(8,128)(2,1)S(1)}, u32[]{:S(2)}, u32[]{:S(2)}) collective-permute-start(bf16[16,1792]{1,0:T(8,128)(2,1)S(1)} %get-tuple-element.57), channel_id=1, source_target_pairs={{0,8},{8,0},{16,24},{24,16},{1,9},{9,1},{17,25},{25,17},{2,10},{10... | collective-permute-start | bytes 172040 | tf_op jit(solution)/shard_map/ppermute | solution.py:17
  27.6 7.3 %collective-permute-start.7 = (bf16[16,1792]{1,0:T(8,128)(2,1)S(1)}, bf16[16,1792]{1,0:T(8,128)(2,1)S(1)}, u32[]{:S(2)}, u32[]{:S(2)}) collective-permute-start(bf16[16,1792]{1,0:T(8,128)(2,1)S(1)} %get-tuple-element.58), channel_id=1, source_target_pairs={{0,16},{8,24},{16,0},{24,8},{1,17},{9,25},{17,1},{25,9},{2,18},{10... | collective-permute-start | bytes 172040 | tf_op jit(solution)/shard_map/ppermute | solution.py:17
  28.1 6.7 %collective-permute-start.8 = (bf16[16,1792]{1,0:T(8,128)(2,1)S(1)}, bf16[16,1792]{1,0:T(8,128)(2,1)S(1)}, u32[]{:S(2)}, u32[]{:S(2)}) collective-permute-start(bf16[16,1792]{1,0:T(8,128)(2,1)S(1)} %get-tuple-element.59), channel_id=1, source_target_pairs={{0,24},{8,16},{16,8},{24,0},{1,25},{9,17},{17,9},{25,1},{2,26},{10... | collective-permute-start | bytes 172040 | tf_op jit(solution)/shard_map/ppermute | solution.py:17
  35.0 4.4 %collective-permute-start.9 = (bf16[16,1920]{1,0:T(8,128)(2,1)S(1)}, bf16[16,1920]{1,0:T(8,128)(2,1)S(1)}, u32[]{:S(2)}, u32[]{:S(2)}) collective-permute-start(bf16[16,1920]{1,0:T(8,128)(2,1)S(1)} %get-tuple-element.61), channel_id=1, source_target_pairs={{0,2},{1,3},{2,0},{3,1},{4,6},{5,7},{6,4},{7,5},{8,10},{9,11},{10,... | collective-permute-start | bytes 184328 | tf_op jit(solution)/shard_map/ppermute | solution.py:17
  35.7 4.8 %collective-permute-start.10 = (bf16[16,1920]{1,0:T(8,128)(2,1)S(1)}, bf16[16,1920]{1,0:T(8,128)(2,1)S(1)}, u32[]{:S(2)}, u32[]{:S(2)}) collective-permute-start(bf16[16,1920]{1,0:T(8,128)(2,1)S(1)} %get-tuple-element.62), channel_id=1, source_target_pairs={{0,4},{1,5},{2,6},{3,7},{4,0},{5,1},{6,2},{7,3},{8,12},{9,13},{10,... | collective-permute-start | bytes 184328 | tf_op jit(solution)/shard_map/ppermute | solution.py:17
  36.3 5.8 %collective-permute-start.11 = (bf16[16,1920]{1,0:T(8,128)(2,1)S(1)}, bf16[16,1920]{1,0:T(8,128)(2,1)S(1)}, u32[]{:S(2)}, u32[]{:S(2)}) collective-permute-start(bf16[16,1920]{1,0:T(8,128)(2,1)S(1)} %get-tuple-element.63), channel_id=1, source_target_pairs={{0,6},{1,7},{2,4},{3,5},{4,2},{5,3},{6,0},{7,1},{8,14},{9,15},{10,... | collective-permute-start | bytes 184328 | tf_op jit(solution)/shard_map/ppermute | solution.py:17
  38.5 4.2 %collective-permute-start.16 = (bf16[4,7168]{1,0:T(4,128)(2,1)S(1)}, bf16[4,7168]{1,0:T(4,128)(2,1)S(1)}, u32[]{:S(2)}, u32[]{:S(2)}) collective-permute-start(bf16[4,7168]{1,0:T(4,128)(2,1)S(1)} %get-tuple-element.71), channel_id=1, source_target_pairs={{0,2},{1,3},{2,0},{3,1},{4,6},{5,7},{6,4},{7,5},{8,10},{9,11},{10,... | collective-permute-start | bytes 172040 | tf_op jit(solution)/shard_map/ppermute | solution.py:17
  39.4 4.2 %collective-permute-start.17 = (bf16[4,7168]{1,0:T(4,128)(2,1)S(1)}, bf16[4,7168]{1,0:T(4,128)(2,1)S(1)}, u32[]{:S(2)}, u32[]{:S(2)}) collective-permute-start(bf16[4,7168]{1,0:T(4,128)(2,1)S(1)} %get-tuple-element.72), channel_id=1, source_target_pairs={{0,4},{1,5},{2,6},{3,7},{4,0},{5,1},{6,2},{7,3},{8,12},{9,13},{10,... | collective-permute-start | bytes 172040 | tf_op jit(solution)/shard_map/ppermute | solution.py:17
  40.5 5.1 %collective-permute-start.18 = (bf16[4,7168]{1,0:T(4,128)(2,1)S(1)}, bf16[4,7168]{1,0:T(4,128)(2,1)S(1)}, u32[]{:S(2)}, u32[]{:S(2)}) collective-permute-start(bf16[4,7168]{1,0:T(4,128)(2,1)S(1)} %get-tuple-element.73), channel_id=1, source_target_pairs={{0,6},{1,7},{2,4},{3,5},{4,2},{5,3},{6,0},{7,1},{8,14},{9,15},{10,... | collective-permute-start | bytes 172040 | tf_op jit(solution)/shard_map/ppermute | solution.py:17
  42.2 9.9 %collective-permute-start.12 = (bf16[16,2048]{1,0:T(8,128)(2,1)S(1)}, bf16[16,2048]{1,0:T(8,128)(2,1)S(1)}, u32[]{:S(2)}, u32[]{:S(2)}) collective-permute-start(bf16[16,2048]{1,0:T(8,128)(2,1)S(1)} %get-tuple-element.64.own_ref), channel_id=1, source_target_pairs={{0,1},{1,0},{2,3},{3,2},{4,5},{5,4},{6,7},{7,6},{8,9},{9,8},{10,11... | collective-permute-start | bytes 196616 | tf_op jit(solution)/shard_map/ppermute | solution.py:17
  45.7 4.2 %collective-permute-start.19 = (bf16[4,7168]{1,0:T(4,128)(2,1)S(1)}, bf16[4,7168]{1,0:T(4,128)(2,1)S(1)}, u32[]{:S(2)}, u32[]{:S(2)}) collective-permute-start(bf16[4,7168]{1,0:T(4,128)(2,1)S(1)} %shard_map.134.refs_0_), channel_id=1, source_target_pairs={{0,8},{8,0},{16,24},{24,16},{1,9},{9,1},{17,25},{25,17},{2,10},{10... | collective-permute-start | bytes 172040 | tf_op jit(solution)/shard_map/ppermute | solution.py:17
  46.7 10.6 %collective-permute-start.5 = (bf16[144,32]{1,0:T(8,128)(2,1)S(1)}, bf16[144,32]{1,0:T(8,128)(2,1)S(1)}, u32[]{:S(2)}, u32[]{:S(2)}) collective-permute-start(bf16[144,32]{1,0:T(8,128)(2,1)S(1)} %get-tuple-element.51), channel_id=1, source_target_pairs={{0,1},{1,0},{2,3},{3,2},{4,5},{5,4},{6,7},{7,6},{8,9},{9,8},{10,11... | collective-permute-start | bytes 27656 | tf_op jit(solution)/shard_map/ppermute | solution.py:17
  49.9 9.9 %collective-permute-start.20 = (bf16[4,7168]{1,0:T(4,128)(2,1)S(1)}, bf16[4,7168]{1,0:T(4,128)(2,1)S(1)}, u32[]{:S(2)}, u32[]{:S(2)}) collective-permute-start(bf16[4,7168]{1,0:T(4,128)(2,1)S(1)} %shard_map.135.refs_4_), channel_id=1, source_target_pairs={{0,16},{8,24},{16,0},{24,8},{1,17},{9,25},{17,1},{25,9},{2,18},{10... | collective-permute-start | bytes 172040 | tf_op jit(solution)/shard_map/ppermute | solution.py:17
  52.8 7.0 %collective-permute-start.13 = (bf16[8,1408]{1,0:T(8,128)(2,1)S(1)}, bf16[8,1408]{1,0:T(8,128)(2,1)S(1)}, u32[]{:S(2)}, u32[]{:S(2)}) collective-permute-start(bf16[8,1408]{1,0:T(8,128)(2,1)S(1)} %get-tuple-element.67), channel_id=1, source_target_pairs={{0,8},{8,0},{16,24},{24,16},{1,9},{9,1},{17,25},{25,17},{2,10},{10... | collective-permute-start | bytes 67592 | tf_op jit(solution)/shard_map/ppermute | solution.py:17
  54.8 5.0 %collective-permute-start.14 = (bf16[8,1408]{1,0:T(8,128)(2,1)S(1)}, bf16[8,1408]{1,0:T(8,128)(2,1)S(1)}, u32[]{:S(2)}, u32[]{:S(2)}) collective-permute-start(bf16[8,1408]{1,0:T(8,128)(2,1)S(1)} %get-tuple-element.68), channel_id=1, source_target_pairs={{0,16},{8,24},{16,0},{24,8},{1,17},{9,25},{17,1},{25,9},{2,18},{10... | collective-permute-start | bytes 67592 | tf_op jit(solution)/shard_map/ppermute | solution.py:17
  54.8 5.6 %collective-permute-start.15 = (bf16[8,1408]{1,0:T(8,128)(2,1)S(1)}, bf16[8,1408]{1,0:T(8,128)(2,1)S(1)}, u32[]{:S(2)}, u32[]{:S(2)}) collective-permute-start(bf16[8,1408]{1,0:T(8,128)(2,1)S(1)} %get-tuple-element.69), channel_id=1, source_target_pairs={{0,24},{8,16},{16,8},{24,0},{1,25},{9,17},{17,9},{25,1},{2,26},{10... | collective-permute-start | bytes 67592 | tf_op jit(solution)/shard_map/ppermute | solution.py:17
  58.2 2.9 %copy-start = (bf16[144,7168]{1,0:T(8,128)(2,1)}, bf16[144,7168]{1,0:T(8,128)(2,1)S(1)}, u32[]{:S(2)}) copy-start(bf16[144,7168]{1,0:T(8,128)(2,1)S(1)} %convolution_convert_fusion.hold_ref) | copy-start | bytes 6193156
  (4 other events, 3.6 us)

commit v2 on v1

--- a/solution.py
+++ b/solution.py
@@ -315,7 +315,7 @@
     module = (iota((1, rows), 1) // tok) % 2 == 1
     share = jnp.where(module, loss_scale * mtp_share, loss_scale).astype(f32)
     peaks, masses, moments, picks = (ev_ref[:, k * rows : (k + 1) * rows] for k in range(4))
-    sender = iota((ev_ref.shape[0], 1), 0) % 2
+    sender = iota((ev_ref.shape[0], 1), 0) // nvoc % 2
 
     def combine(which):
         mine = sender == which
@@ -452,12 +452,14 @@
     pieces = [gain_piece[:, c : c + hdim] for c in range(0, cols, hdim)]
     pieces += [jnp.zeros((1, hdim), f32)] * (tok_voc - len(pieces))
     gains = jnp.concatenate(pieces, axis=0)
-    gains = gains.astype(bf16)
+    high = gains.astype(bf16)
+    low = (gains - high.astype(f32)).astype(bf16)
     for k, out in enumerate(parcels):
         block = scratch[pl.ds(pl.multiple_of((voc ^ k) * tok_voc, tok_voc), tok_voc), :]
         out[:, :strip] = mine
         out[:, strip : strip + hdim] = block.astype(bf16)
-        out[:, strip + hdim :] = gains
+        out[:, strip + hdim : strip + 2 * hdim] = high
+        out[:, strip + 2 * hdim :] = low
     line, spot = iota((half, nmod), 0), iota((half, nmod), 1)
     owner = line // tok
     same = spot == ((owner // 2) ^ chip) * tok + line % tok
@@ -484,7 +486,7 @@
         for f in range(fold):
             at = pl.ds(pl.multiple_of((voc ^ k) * cols + f * strip, 128), strip)
             res_ref[:, at] = part[f * tok : (f + 1) * tok, :strip].astype(bf16)
-        gains = part[:, strip + hdim :]
+        gains = part[:, strip + hdim : strip + 2 * hdim] + part[:, strip + 2 * hdim :]
         for i in range(cols // hdim):
             at = pl.ds(pl.multiple_of((voc ^ k) * cols + i * hdim, 128), hdim)
             gain_ref[:, at] = gains[i : i + 1]
@@ -548,7 +550,7 @@
     )
     raw_near = swap(raw, "rows", 1)
     everyone = lax.all_to_all(
-        stats, ("vocab", "rows"), split_axis=0, concat_axis=0, tiled=True
+        stats, ("rows", "vocab"), split_axis=0, concat_axis=0, tiled=True
     )
     grads, grads_away, dot_mean, *pieces = kernel_call(
         part(loss_kernel, tok, nvoc),
@@ -598,7 +600,7 @@
     residual, values, *parcels = kernel_call(
         part(last_kernel, tok),
         [((ntok, cols), bf16), ((ntok, hdim), bf16)]
-        + [((tok_voc, cols * tok // tok_voc + 2 * hdim), bf16)] * nvoc,
+        + [((tok_voc, cols * tok // tok_voc + 3 * hdim), bf16)] * nvoc,
         raw,
         raw_near,
         inverse,

time: 61.4 us -> 61.1 us (level)
  starting transfers between devices: 23.1 us -> 21.8 us
  waiting for transfers between devices: 13.7 us -> 14.6 us
    ppermute x21, starting transfers between devices: 23.1 us -> 21.8 us  [swap(): return lax.ppermute(x, axis, [(i, i ^ k) for i in range(n)])]
    ppermute x21, waiting for transfers between devices: 13.7 us -> 14.6 us  [swap(): return lax.ppermute(x, axis, [(i, i ^ k) for i in range(n)])]
where the time goes in v2:
time: 61.1 us; the launch traced here: 60.8 us
  starting transfers between devices  21.8 us (36%)
  waiting for transfers between devices  14.6 us (24%)
  blocking collectives  12.2 us (20%)
  Pallas kernels  6.31 us (10%)
  local copies, waits for them, and re-layouts  3.61 us (6%)
  other arithmetic  0.91 us (1%)
  between operations  0.74 us (1%)
  matrix products  0.68 us (1%)
    ppermute x21, starting transfers between devices, swap(): return lax.ppermute(x, axis, [(i, i ^ k) for i in range(n)])  21.8 us
    ppermute x21, waiting for transfers between devices, swap(): return lax.ppermute(x, axis, [(i, i ^ k) for i in range(n)])  14.6 us
    all_to_all x1, blocking collectives, local(): lax.all_to_all(stats, ('rows', 'vocab'), split_axis=0, concat_axis=0, til...  12.2 us
    pallas_call x11, Pallas kernels, kernel_call(): pl.pallas_call(body, in_specs=[hbm if k in away else vmem for k in range(...  6.31 us
    unnamed x14, local copies, waits for them, and re-layouts  3.61 us
  transfers between devices with their start and end apart: 21, of which 11 were waited for; matrix products, arithmetic and copies ran while one was open for 3% of the time, Pallas kernels for 7%

profile of v2, /device:TPU:0, one launch (start us, length us, event | category | flops | bytes accessed | tf_op | source)
XLA Modules:
  0.0 60.8 jit_solution(6506058007228109005)
XLA Ops:
  1.2 0.9 %pad_maximum_fusion.refs_0_ = bf16[8,7168]{1,0:T(8,128)(2,1)S(1)} fusion(bf16[4,7168]{1,0:T(4,128)(2,1)} %param.9, bf16[4,7168]{1,0:T(4,128)(2,1)} %param.8), kind=kLoop, calls=%fused_computation.1 | loop fusion | flops 229376 | bytes 229376 | tf_op jit(solution)/shard_map/concatenate | solution.py:525
  2.1 3.5 %collective-permute-start.2 = (bf16[8,7168]{1,0:T(8,128)(2,1)S(1)}, bf16[8,7168]{1,0:T(8,128)(2,1)S(1)}, u32[]{:S(2)}, u32[]{:S(2)}) collective-permute-start(bf16[8,7168]{1,0:T(8,128)(2,1)S(1)} %pad_maximum_fusion.refs_0_), channel_id=1, source_target_pairs={{0,6},{1,7},{2,4},{3,5},{4,2},{5,3},{6,0},{7,1},{8,14},{9,15},{10,... | collective-permute-start | bytes 344072 | tf_op jit(solution)/shard_map/ppermute | solution.py:17
  6.3 1.6 %copy-done.1 = bf16[144,7168]{1,0:T(8,128)(2,1)S(1)} copy-done((bf16[144,7168]{1,0:T(8,128)(2,1)S(1)}, bf16[144,7168]{1,0:T(8,128)(2,1)}, u32[]{:S(2)}) %copy-start.1) | copy-done | bytes 2064408
  7.8 0.7 %copy-done.4 = bf16[7168]{0:T(1024)(128)(2,1)S(1)} copy-done((bf16[7168]{0:T(1024)(128)(2,1)S(1)}, bf16[7168]{0:T(1024)(128)(2,1)}, u32[]{:S(2)}) %copy-start.4) | copy-done | bytes 14360
  10.0 1.8 %collective-permute-done.1.refs_2_ = bf16[8,7168]{1,0:T(8,128)(2,1)S(1)} collective-permute-done((bf16[8,7168]{1,0:T(8,128)(2,1)S(1)}, bf16[8,7168]{1,0:T(8,128)(2,1)S(1)}, u32[]{:S(2)}, u32[]{:S(2)}) %collective-permute-start.1) | collective-permute-done | bytes 114720 | tf_op jit(solution)/shard_map/ppermute | solution.py:17
  12.2 1.6 %shard_map.128 = (bf16[32,7296]{1,0:T(8,128)(2,1)S(1)}, bf16[32,7168]{1,0:T(8,128)(2,1)S(1)}, f32[288,32]{1,0:T(8,128)S(1)}, f32[32,1]{1,0:T(8,128)S(1)}, f32[32,128]{1,0:T(8,128)S(1)}) custom-call(bf16[8,7168]{1,0:T(8,128)(2,1)S(1)} %pad_maximum_fusion.refs_0_, bf16[8,7168]{1,0:T(8,128)(2,1)S(1)} %collective-permute-done.refs_1_, ...), custom_call_target="tpu_custom_call" | custom-call | tf_op jit(solution)/shard_map/pallas_call | solution.py:204
  13.8 12.2 %all_to_all.11 = f32[32,1,128]{2,1,0:T(1,128)S(1)} all-to-all(f32[32,1,128]{2,1,0:T(1,128)S(1)} %bitcast.11), channel_id=1, replica_groups=mesh['vocab'=4,'rows'=8] {'rows','vocab'}, dimensions={0} | all-to-all | bytes 32768 | tf_op jit(solution)/shard_map/all_to_all | solution.py:552
  26.0 0.9 %shard_map.129 = (bf16[144,32]{1,0:T(8,128)(2,1)S(1)}, bf16[144,32]{1,0:T(8,128)(2,1)S(1)}, f32[32,1]{1,0:T(8,128)S(1)}, bf16[16,1792]{1,0:T(8,128)(2,1)S(1)}, b...) custom-call(f32[32,128]{1,0:T(8,128)S(1)} %bitcast.10, ...), custom_call_target="tpu_custom_call" | custom-call | tf_op jit(solution)/shard_map/pallas_call | solution.py:204
  28.1 3.3 %collective-permute-start.8 = (bf16[16,1792]{1,0:T(8,128)(2,1)S(1)}, bf16[16,1792]{1,0:T(8,128)(2,1)S(1)}, u32[]{:S(2)}, u32[]{:S(2)}) collective-permute-start(bf16[16,1792]{1,0:T(8,128)(2,1)S(1)} %get-tuple-element.59), channel_id=1, source_target_pairs={{0,24},{8,16},{16,8},{24,0},{1,25},{9,17},{17,9},{25,1},{2,26},{10... | collective-permute-start | bytes 172040 | tf_op jit(solution)/shard_map/ppermute | solution.py:17
  31.8 3.1 %collective-permute-done.7.refs_2_ = bf16[16,1792]{1,0:T(8,128)(2,1)S(1)} collective-permute-done((bf16[16,1792]{1,0:T(8,128)(2,1)S(1)}, bf16[16,1792]{1,0:T(8,128)(2,1)S(1)}, u32[]{:S(2)}, u32[]{:S(2)}) %collective-permute-start.7) | collective-permute-done | bytes 57376 | tf_op jit(solution)/shard_map/ppermute | solution.py:17
  36.2 2.4 %collective-permute-start.11 = (bf16[16,1920]{1,0:T(8,128)(2,1)S(1)}, bf16[16,1920]{1,0:T(8,128)(2,1)S(1)}, u32[]{:S(2)}, u32[]{:S(2)}) collective-permute-start(bf16[16,1920]{1,0:T(8,128)(2,1)S(1)} %get-tuple-element.63), channel_id=1, source_target_pairs={{0,6},{1,7},{2,4},{3,5},{4,2},{5,3},{6,0},{7,1},{8,14},{9,15},{10,... | collective-permute-start | bytes 184328 | tf_op jit(solution)/shard_map/ppermute | solution.py:17
  40.6 1.6 %collective-permute-start.18 = (bf16[4,7168]{1,0:T(4,128)(2,1)S(1)}, bf16[4,7168]{1,0:T(4,128)(2,1)S(1)}, u32[]{:S(2)}, u32[]{:S(2)}) collective-permute-start(bf16[4,7168]{1,0:T(4,128)(2,1)S(1)} %get-tuple-element.73), channel_id=1, source_target_pairs={{0,6},{1,7},{2,4},{3,5},{4,2},{5,3},{6,0},{7,1},{8,14},{9,15},{10,... | collective-permute-start | bytes 172040 | tf_op jit(solution)/shard_map/ppermute | solution.py:17
  42.8 0.7 %collective-permute-done.17.refs_2_ = bf16[4,7168]{1,0:T(4,128)(2,1)S(1)} collective-permute-done((bf16[4,7168]{1,0:T(4,128)(2,1)S(1)}, bf16[4,7168]{1,0:T(4,128)(2,1)S(1)}, u32[]{:S(2)}, u32[]{:S(2)}) %collective-permute-start.17) | collective-permute-done | bytes 57376 | tf_op jit(solution)/shard_map/ppermute | solution.py:17
  43.5 2.1 %collective-permute-done.18.refs_3_ = bf16[4,7168]{1,0:T(4,128)(2,1)S(1)} collective-permute-done((bf16[4,7168]{1,0:T(4,128)(2,1)S(1)}, bf16[4,7168]{1,0:T(4,128)(2,1)S(1)}, u32[]{:S(2)}, u32[]{:S(2)}) %collective-permute-start.18) | collective-permute-done | bytes 57376 | tf_op jit(solution)/shard_map/ppermute | solution.py:17
  45.7 0.9 %collective-permute-start.19 = (bf16[4,7168]{1,0:T(4,128)(2,1)S(1)}, bf16[4,7168]{1,0:T(4,128)(2,1)S(1)}, u32[]{:S(2)}, u32[]{:S(2)}) collective-permute-start(bf16[4,7168]{1,0:T(4,128)(2,1)S(1)} %shard_map.134.refs_0_), channel_id=1, source_target_pairs={{0,8},{8,0},{16,24},{24,16},{1,9},{9,1},{17,25},{25,17},{2,10},{10... | collective-permute-start | bytes 172040 | tf_op jit(solution)/shard_map/ppermute | solution.py:17
  46.6 3.4 %collective-permute-done.19.refs_1_ = bf16[4,7168]{1,0:T(4,128)(2,1)S(1)} collective-permute-done((bf16[4,7168]{1,0:T(4,128)(2,1)S(1)}, bf16[4,7168]{1,0:T(4,128)(2,1)S(1)}, u32[]{:S(2)}, u32[]{:S(2)}) %collective-permute-start.19) | collective-permute-done | bytes 57376 | tf_op jit(solution)/shard_map/ppermute | solution.py:17
  50.0 0.9 %collective-permute-start.20 = (bf16[4,7168]{1,0:T(4,128)(2,1)S(1)}, bf16[4,7168]{1,0:T(4,128)(2,1)S(1)}, u32[]{:S(2)}, u32[]{:S(2)}) collective-permute-start(bf16[4,7168]{1,0:T(4,128)(2,1)S(1)} %shard_map.135.refs_4_), channel_id=1, source_target_pairs={{0,16},{8,24},{16,0},{24,8},{1,17},{9,25},{17,1},{25,9},{2,18},{10... | collective-permute-start | bytes 172040 | tf_op jit(solution)/shard_map/ppermute | solution.py:17
  51.5 2.1 %collective-permute-start.13 = (bf16[8,1664]{1,0:T(8,128)(2,1)S(1)}, bf16[8,1664]{1,0:T(8,128)(2,1)S(1)}, u32[]{:S(2)}, u32[]{:S(2)}) collective-permute-start(bf16[8,1664]{1,0:T(8,128)(2,1)S(1)} %get-tuple-element.67), channel_id=1, source_target_pairs={{0,8},{8,0},{16,24},{24,16},{1,9},{9,1},{17,25},{25,17},{2,10},{10... | collective-permute-start | bytes 79880 | tf_op jit(solution)/shard_map/ppermute | solution.py:17
  53.6 0.9 %collective-permute-start.14 = (bf16[8,1664]{1,0:T(8,128)(2,1)S(1)}, bf16[8,1664]{1,0:T(8,128)(2,1)S(1)}, u32[]{:S(2)}, u32[]{:S(2)}) collective-permute-start(bf16[8,1664]{1,0:T(8,128)(2,1)S(1)} %get-tuple-element.68), channel_id=1, source_target_pairs={{0,16},{8,24},{16,0},{24,8},{1,17},{9,25},{17,1},{25,9},{2,18},{10... | collective-permute-start | bytes 79880 | tf_op jit(solution)/shard_map/ppermute | solution.py:17
  54.5 1.6 %collective-permute-start.15 = (bf16[8,1664]{1,0:T(8,128)(2,1)S(1)}, bf16[8,1664]{1,0:T(8,128)(2,1)S(1)}, u32[]{:S(2)}, u32[]{:S(2)}) collective-permute-start(bf16[8,1664]{1,0:T(8,128)(2,1)S(1)} %get-tuple-element.69), channel_id=1, source_target_pairs={{0,24},{8,16},{16,8},{24,0},{1,25},{9,17},{17,9},{25,1},{2,26},{10... | collective-permute-start | bytes 79880 | tf_op jit(solution)/shard_map/ppermute | solution.py:17
  56.3 0.7 %convolution_convert_fusion.hold_ref = bf16[144,7168]{1,0:T(8,128)(2,1)S(1)} fusion(bf16[144,64]{1,0:T(8,128)(2,1)S(1)} %get-tuple-element.52, bf16[64,7168]{1,0:T(8,128)(2,1)S(1)} %get-tuple-element.53), kind=kOutput, calls=%fused_computation | convolution fusion | flops 133152768 | bytes 3000320 | tf_op jit(solution)/shard_map/dot_general | solution.py:580
  57.0 1.6 %shard_map.137 = bf16[256,1792]{1,0:T(8,128)(2,1)} custom-call(bf16[32,256]{1,0:T(8,128)(2,1)S(1)} %get-tuple-element.78.val_ref, bf16[32,1792]{1,0:T(8,128)(2,1)S(1)} %get-tuple-element.79.res_ref), custom_call_target="tpu_custom_call" | custom-call | tf_op jit(solution)/shard_map/pallas_call | solution.py:204
  58.6 1.5 %collective-permute-done.15.refs_3_ = bf16[8,1664]{1,0:T(8,128)(2,1)S(1)} collective-permute-done((bf16[8,1664]{1,0:T(8,128)(2,1)S(1)}, bf16[8,1664]{1,0:T(8,128)(2,1)S(1)}, u32[]{:S(2)}, u32[]{:S(2)}) %collective-permute-start.15) | collective-permute-done | bytes 26656 | tf_op jit(solution)/shard_map/ppermute | solution.py:17
  60.1 0.7 %shard_map.136 = (bf16[4,7168]{1,0:T(4,128)(2,1)}, bf16[4,7168]{1,0:T(4,128)(2,1)}, f32[1,7168]{1,0:T(1,128)}, bf16[8,2,128]{2,1,0:T(2,128)(2,1)}) custom-call(bf16[144,7168]{1,0:T(8,128)(2,1)S(1)} %convolution_convert_fusion.hold_ref, bf16[8,1664]{1,0:T(8,128)(2,1)S(1)} %get-tuple-element.66.refs_0_, bf16[8,1664]{1,0:T(8,128)(2,1)S(1)} %collective-permute-done.13.refs_1_, ...), custom_call_target="tpu_custom_call" | custom-call | tf_op jit(solution)/shard_map/pallas_call | solution.py:204
  (46 shorter events, 9.5 us)
Async XLA Ops:
  0.6 11.5 %collective-permute-start.3 = (bf16[144,7168]{1,0:T(8,128)(2,1)}, bf16[144,7168]{1,0:T(8,128)(2,1)S(1)}, u32[]{:S(2)}, u32[]{:S(2)}) collective-permute-start(bf16[144,7168]{1,0:T(8,128)(2,1)} %w_src.1), channel_id=1, source_target_pairs={{0,1},{1,0},{2,3},{3,2},{4,5},{5,4},{6,7},{7,6},{8,9},{9,8},{10,11... | collective-permute-start | bytes 6193160 | tf_op jit(solution)/shard_map/ppermute | solution.py:17
  2.1 7.9 %collective-permute-start.2 = (bf16[8,7168]{1,0:T(8,128)(2,1)S(1)}, bf16[8,7168]{1,0:T(8,128)(2,1)S(1)}, u32[]{:S(2)}, u32[]{:S(2)}) collective-permute-start(bf16[8,7168]{1,0:T(8,128)(2,1)S(1)} %pad_maximum_fusion.refs_0_), channel_id=1, source_target_pairs={{0,6},{1,7},{2,4},{3,5},{4,2},{5,3},{6,0},{7,1},{8,14},{9,15},{10,... | collective-permute-start | bytes 344072 | tf_op jit(solution)/shard_map/ppermute | solution.py:17
  5.6 6.3 %collective-permute-start.1 = (bf16[8,7168]{1,0:T(8,128)(2,1)S(1)}, bf16[8,7168]{1,0:T(8,128)(2,1)S(1)}, u32[]{:S(2)}, u32[]{:S(2)}) collective-permute-start(bf16[8,7168]{1,0:T(8,128)(2,1)S(1)} %pad_maximum_fusion.refs_0_), channel_id=1, source_target_pairs={{0,4},{1,5},{2,6},{3,7},{4,0},{5,1},{6,2},{7,3},{8,12},{9,13},{10,... | collective-permute-start | bytes 344072 | tf_op jit(solution)/shard_map/ppermute | solution.py:17
  6.1 6.0 %collective-permute-start = (bf16[8,7168]{1,0:T(8,128)(2,1)S(1)}, bf16[8,7168]{1,0:T(8,128)(2,1)S(1)}, u32[]{:S(2)}, u32[]{:S(2)}) collective-permute-start(bf16[8,7168]{1,0:T(8,128)(2,1)S(1)} %pad_maximum_fusion.refs_0_), channel_id=1, source_target_pairs={{0,2},{1,3},{2,0},{3,1},{4,6},{5,7},{6,4},{7,5},{8,10},{9,11},{10,... | collective-permute-start | bytes 344072 | tf_op jit(solution)/shard_map/ppermute | solution.py:17
  13.8 37.1 %collective-permute-start.4 = (bf16[32,7296]{1,0:T(8,128)(2,1)S(1)}, bf16[32,7296]{1,0:T(8,128)(2,1)S(1)}, u32[]{:S(2)}, u32[]{:S(2)}) collective-permute-start(bf16[32,7296]{1,0:T(8,128)(2,1)S(1)} %get-tuple-element.46.raw_ref), channel_id=1, source_target_pairs={{0,1},{1,0},{2,3},{3,2},{4,5},{5,4},{6,7},{7,6},{8,9},{9,8},{10,11... | collective-permute-start | bytes 1400840 | tf_op jit(solution)/shard_map/ppermute | solution.py:17
  26.0 8.9 %copy-start.3 = (bf16[4,16,128]{2,1,0:T(8,128)(2,1)S(1)}, bf16[4,16,128]{2,1,0:T(8,128)(2,1)}, u32[]{:S(2)}) copy-start(bf16[4,16,128]{2,1,0:T(8,128)(2,1)} %attn_ref.1) | copy-start | bytes 49156
  26.0 24.9 %copy-start.2 = (bf16[256,1792]{1,0:T(8,128)(2,1)S(1)}, bf16[256,1792]{1,0:T(8,128)(2,1)}, u32[]{:S(2)}) copy-start(bf16[256,1792]{1,0:T(8,128)(2,1)} %proj_ref.1) | copy-start | bytes 2752516
  26.9 4.9 %collective-permute-start.6 = (bf16[16,1792]{1,0:T(8,128)(2,1)S(1)}, bf16[16,1792]{1,0:T(8,128)(2,1)S(1)}, u32[]{:S(2)}, u32[]{:S(2)}) collective-permute-start(bf16[16,1792]{1,0:T(8,128)(2,1)S(1)} %get-tuple-element.57), channel_id=1, source_target_pairs={{0,8},{8,0},{16,24},{24,16},{1,9},{9,1},{17,25},{25,17},{2,10},{10... | collective-permute-start | bytes 172040 | tf_op jit(solution)/shard_map/ppermute | solution.py:17
  27.5 7.4 %collective-permute-start.7 = (bf16[16,1792]{1,0:T(8,128)(2,1)S(1)}, bf16[16,1792]{1,0:T(8,128)(2,1)S(1)}, u32[]{:S(2)}, u32[]{:S(2)}) collective-permute-start(bf16[16,1792]{1,0:T(8,128)(2,1)S(1)} %get-tuple-element.58), channel_id=1, source_target_pairs={{0,16},{8,24},{16,0},{24,8},{1,17},{9,25},{17,1},{25,9},{2,18},{10... | collective-permute-start | bytes 172040 | tf_op jit(solution)/shard_map/ppermute | solution.py:17
  28.1 6.8 %collective-permute-start.8 = (bf16[16,1792]{1,0:T(8,128)(2,1)S(1)}, bf16[16,1792]{1,0:T(8,128)(2,1)S(1)}, u32[]{:S(2)}, u32[]{:S(2)}) collective-permute-start(bf16[16,1792]{1,0:T(8,128)(2,1)S(1)} %get-tuple-element.59), channel_id=1, source_target_pairs={{0,24},{8,16},{16,8},{24,0},{1,25},{9,17},{17,9},{25,1},{2,26},{10... | collective-permute-start | bytes 172040 | tf_op jit(solution)/shard_map/ppermute | solution.py:17
  35.1 4.3 %collective-permute-start.9 = (bf16[16,1920]{1,0:T(8,128)(2,1)S(1)}, bf16[16,1920]{1,0:T(8,128)(2,1)S(1)}, u32[]{:S(2)}, u32[]{:S(2)}) collective-permute-start(bf16[16,1920]{1,0:T(8,128)(2,1)S(1)} %get-tuple-element.61), channel_id=1, source_target_pairs={{0,2},{1,3},{2,0},{3,1},{4,6},{5,7},{6,4},{7,5},{8,10},{9,11},{10,... | collective-permute-start | bytes 184328 | tf_op jit(solution)/shard_map/ppermute | solution.py:17
  35.7 4.8 %collective-permute-start.10 = (bf16[16,1920]{1,0:T(8,128)(2,1)S(1)}, bf16[16,1920]{1,0:T(8,128)(2,1)S(1)}, u32[]{:S(2)}, u32[]{:S(2)}) collective-permute-start(bf16[16,1920]{1,0:T(8,128)(2,1)S(1)} %get-tuple-element.62), channel_id=1, source_target_pairs={{0,4},{1,5},{2,6},{3,7},{4,0},{5,1},{6,2},{7,3},{8,12},{9,13},{10,... | collective-permute-start | bytes 184328 | tf_op jit(solution)/shard_map/ppermute | solution.py:17
  36.2 5.9 %collective-permute-start.11 = (bf16[16,1920]{1,0:T(8,128)(2,1)S(1)}, bf16[16,1920]{1,0:T(8,128)(2,1)S(1)}, u32[]{:S(2)}, u32[]{:S(2)}) collective-permute-start(bf16[16,1920]{1,0:T(8,128)(2,1)S(1)} %get-tuple-element.63), channel_id=1, source_target_pairs={{0,6},{1,7},{2,4},{3,5},{4,2},{5,3},{6,0},{7,1},{8,14},{9,15},{10,... | collective-permute-start | bytes 184328 | tf_op jit(solution)/shard_map/ppermute | solution.py:17
  38.6 4.2 %collective-permute-start.16 = (bf16[4,7168]{1,0:T(4,128)(2,1)S(1)}, bf16[4,7168]{1,0:T(4,128)(2,1)S(1)}, u32[]{:S(2)}, u32[]{:S(2)}) collective-permute-start(bf16[4,7168]{1,0:T(4,128)(2,1)S(1)} %get-tuple-element.71), channel_id=1, source_target_pairs={{0,2},{1,3},{2,0},{3,1},{4,6},{5,7},{6,4},{7,5},{8,10},{9,11},{10,... | collective-permute-start | bytes 172040 | tf_op jit(solution)/shard_map/ppermute | solution.py:17
  39.4 4.2 %collective-permute-start.17 = (bf16[4,7168]{1,0:T(4,128)(2,1)S(1)}, bf16[4,7168]{1,0:T(4,128)(2,1)S(1)}, u32[]{:S(2)}, u32[]{:S(2)}) collective-permute-start(bf16[4,7168]{1,0:T(4,128)(2,1)S(1)} %get-tuple-element.72), channel_id=1, source_target_pairs={{0,4},{1,5},{2,6},{3,7},{4,0},{5,1},{6,2},{7,3},{8,12},{9,13},{10,... | collective-permute-start | bytes 172040 | tf_op jit(solution)/shard_map/ppermute | solution.py:17
  40.6 5.1 %collective-permute-start.18 = (bf16[4,7168]{1,0:T(4,128)(2,1)S(1)}, bf16[4,7168]{1,0:T(4,128)(2,1)S(1)}, u32[]{:S(2)}, u32[]{:S(2)}) collective-permute-start(bf16[4,7168]{1,0:T(4,128)(2,1)S(1)} %get-tuple-element.73), channel_id=1, source_target_pairs={{0,6},{1,7},{2,4},{3,5},{4,2},{5,3},{6,0},{7,1},{8,14},{9,15},{10,... | collective-permute-start | bytes 172040 | tf_op jit(solution)/shard_map/ppermute | solution.py:17
  42.3 8.6 %collective-permute-start.12 = (bf16[16,2048]{1,0:T(8,128)(2,1)S(1)}, bf16[16,2048]{1,0:T(8,128)(2,1)S(1)}, u32[]{:S(2)}, u32[]{:S(2)}) collective-permute-start(bf16[16,2048]{1,0:T(8,128)(2,1)S(1)} %get-tuple-element.64.own_ref), channel_id=1, source_target_pairs={{0,1},{1,0},{2,3},{3,2},{4,5},{5,4},{6,7},{7,6},{8,9},{9,8},{10,11... | collective-permute-start | bytes 196616 | tf_op jit(solution)/shard_map/ppermute | solution.py:17
  45.7 4.2 %collective-permute-start.19 = (bf16[4,7168]{1,0:T(4,128)(2,1)S(1)}, bf16[4,7168]{1,0:T(4,128)(2,1)S(1)}, u32[]{:S(2)}, u32[]{:S(2)}) collective-permute-start(bf16[4,7168]{1,0:T(4,128)(2,1)S(1)} %shard_map.134.refs_0_), channel_id=1, source_target_pairs={{0,8},{8,0},{16,24},{24,16},{1,9},{9,1},{17,25},{25,17},{2,10},{10... | collective-permute-start | bytes 172040 | tf_op jit(solution)/shard_map/ppermute | solution.py:17
  46.5 9.5 %collective-permute-start.5 = (bf16[144,32]{1,0:T(8,128)(2,1)S(1)}, bf16[144,32]{1,0:T(8,128)(2,1)S(1)}, u32[]{:S(2)}, u32[]{:S(2)}) collective-permute-start(bf16[144,32]{1,0:T(8,128)(2,1)S(1)} %get-tuple-element.51), channel_id=1, source_target_pairs={{0,1},{1,0},{2,3},{3,2},{4,5},{5,4},{6,7},{7,6},{8,9},{9,8},{10,11... | collective-permute-start | bytes 27656 | tf_op jit(solution)/shard_map/ppermute | solution.py:17
  50.0 8.7 %collective-permute-start.20 = (bf16[4,7168]{1,0:T(4,128)(2,1)S(1)}, bf16[4,7168]{1,0:T(4,128)(2,1)S(1)}, u32[]{:S(2)}, u32[]{:S(2)}) collective-permute-start(bf16[4,7168]{1,0:T(4,128)(2,1)S(1)} %shard_map.135.refs_4_), channel_id=1, source_target_pairs={{0,16},{8,24},{16,0},{24,8},{1,17},{9,25},{17,1},{25,9},{2,18},{10... | collective-permute-start | bytes 172040 | tf_op jit(solution)/shard_map/ppermute | solution.py:17
  51.5 7.1 %collective-permute-start.13 = (bf16[8,1664]{1,0:T(8,128)(2,1)S(1)}, bf16[8,1664]{1,0:T(8,128)(2,1)S(1)}, u32[]{:S(2)}, u32[]{:S(2)}) collective-permute-start(bf16[8,1664]{1,0:T(8,128)(2,1)S(1)} %get-tuple-element.67), channel_id=1, source_target_pairs={{0,8},{8,0},{16,24},{24,16},{1,9},{9,1},{17,25},{25,17},{2,10},{10... | collective-permute-start | bytes 79880 | tf_op jit(solution)/shard_map/ppermute | solution.py:17
  53.6 5.0 %collective-permute-start.14 = (bf16[8,1664]{1,0:T(8,128)(2,1)S(1)}, bf16[8,1664]{1,0:T(8,128)(2,1)S(1)}, u32[]{:S(2)}, u32[]{:S(2)}) collective-permute-start(bf16[8,1664]{1,0:T(8,128)(2,1)S(1)} %get-tuple-element.68), channel_id=1, source_target_pairs={{0,16},{8,24},{16,0},{24,8},{1,17},{9,25},{17,1},{25,9},{2,18},{10... | collective-permute-start | bytes 79880 | tf_op jit(solution)/shard_map/ppermute | solution.py:17
  54.5 5.6 %collective-permute-start.15 = (bf16[8,1664]{1,0:T(8,128)(2,1)S(1)}, bf16[8,1664]{1,0:T(8,128)(2,1)S(1)}, u32[]{:S(2)}, u32[]{:S(2)}) collective-permute-start(bf16[8,1664]{1,0:T(8,128)(2,1)S(1)} %get-tuple-element.69), channel_id=1, source_target_pairs={{0,24},{8,16},{16,8},{24,0},{1,25},{9,17},{17,9},{25,1},{2,26},{10... | collective-permute-start | bytes 79880 | tf_op jit(solution)/shard_map/ppermute | solution.py:17
  57.0 3.8 %copy-start = (bf16[144,7168]{1,0:T(8,128)(2,1)}, bf16[144,7168]{1,0:T(8,128)(2,1)S(1)}, u32[]{:S(2)}) copy-start(bf16[144,7168]{1,0:T(8,128)(2,1)S(1)} %convolution_convert_fusion.hold_ref) | copy-start | bytes 6193156
  (4 other events, 3.6 us)
